TPU v7x, 512 devices: a whole 4x4x16 slice. The times are simulated.
512 devices in a mesh: tf: 32 (over x, y, core), bl: 16 (over z).
Axes of the slice: x: 4, y: 4, z: 16, core: 2. Of those that a mesh axis runs over, the one named last changes fastest.
Arguments:
- gains: float32 [2, 64, 1024], P(None, 'tf', 'bl'), may hold values from -5 to 5
- gain_tan: float32 [2, 64, 1024], P(None, 'tf', 'bl'), may hold values from -6 to 6
- group_vis: float32 [2, 64, 1984], P(None, 'tf', 'bl'), may hold values from -6 to 6
- group_tan: float32 [2, 64, 1984], P(None, 'tf', 'bl'), may hold values from -6 to 6
- dish_of: int32 [1024], replicated, may hold values from 0 to 1023, each once
- group_of: int32 [1984], replicated, may hold values from 0 to 1983, each once
- block_list: int32 [528, 2], P('bl'), may hold values from 0 to 31, as said below
- weights: int32 [528, 1024], P('bl'), may hold values from 0 to 4
Outputs:
- gain_update: float32 [2, 64, 1024], P(None, 'tf', 'bl')
- group_update: float32 [2, 64, 1984], P(None, 'tf', 'bl')
Inputs may be any that keep to these rules, and one draw needn't show every extreme that they name: `block_list`: each pair 0 <= r1 <= r2 < 32 stands in exactly one slot.
All inputs are finite; a program needn't handle non-finite values.
Results may differ from a plain program's by a relative error of at most 0.0003.
Values sent between devices are 32-bit elements; how exact they have to be, the bound alone decides.
No kernel may reach another device: no remote copies, remote signals or barrier semaphores. Data moves between devices by JAX's collectives and lax.ppermute only.
A program may use at most 64 MiB of HBM per device.

v0:
```python
import jax
import jax.numpy as jnp
from jax import lax
from jax.sharding import PartitionSpec as P

ROWS = 32
COLS = 32
DISHES = 1024
GROUPS = 1984


prior_weight = 0.5


def rows_first(arrays, axis, dims):
    turned = [jnp.moveaxis(a, dim, 0) for a, dim in zip(arrays, dims)]
    widths = [t[0].size for t in turned]
    both = jnp.concatenate([t.reshape(-1, w) for t, w in zip(turned, widths)], axis=1)
    out = lax.all_gather(both, axis, axis=0, tiled=True)
    blocks = jnp.split(out, [sum(widths[:k]) for k in range(1, len(widths))], axis=1)
    return tuple(
        (
            jnp.moveaxis(b.reshape(-1, *t.shape[1:]), 0, dim)
            for b, t, dim in zip(blocks, turned, dims)
        )
    )


def from_everyone(x, axis):
    peers = lax.axis_size(axis)
    return lax.all_to_all(jnp.broadcast_to(x[None], (peers, *x.shape)), axis, 0, 0, tiled=True)


def of_everyone(x, axis):
    return from_everyone(x, axis).sum(axis=0)


def packed_total(arrays, axis):
    ravelled, at, gathered = (jnp.concatenate([a.reshape(-1) for a in arrays]), 0, [])
    subtotal = of_everyone(ravelled, axis)
    for a in arrays:
        gathered.append(subtotal[at : at + a.size].reshape(a.shape))
        at += a.size
    return tuple(gathered)


def extended(x, sides, width):
    for axis, dim in sides:
        peers, length = (lax.axis_size(axis), x.shape[dim])
        up = [(i, (i + 1) % peers) for i in range(peers - 1)]
        down = [(j, i) for i, j in up]
        last = lax.slice_in_dim(x, length - width, length, axis=dim)
        first = lax.slice_in_dim(x, 0, width, axis=dim)
        before = lax.ppermute(last, axis, up)
        after = lax.ppermute(first, axis, down)
        x = jnp.concatenate([before, x, after], axis=dim)
    return x


def times_complex(left, right):
    return jnp.stack(
        [left[0] * right[0] - left[1] * right[1], left[0] * right[1] + left[1] * right[0]]
    )


def conjugate(values):
    return jnp.stack([values[0], -values[1]])


def select_rows(table, onehot):
    return jnp.einsum("pcrk,br->pcbk", table, onehot, precision=lax.Precision.HIGHEST)


def local(gains, gain_tan, group_vis, group_tan, dish_of, group_of, block_list, weights):
    columns = COLS
    offsets = 2 * columns - 1
    chans = gains.shape[1]
    dish_count = gains.shape[2]
    group_count = group_vis.shape[2]
    slots = block_list.shape[0]
    all_gain, all_tan = rows_first((gains, gain_tan), "bl", (2, 2))
    all_vis, all_gtan = rows_first((group_vis, group_tan), "bl", (2, 2))
    dish_hot = (jnp.arange(DISHES, dtype=jnp.int32)[:, None] == dish_of[None, :]).astype(
        jnp.float32
    )
    group_hot = (jnp.arange(GROUPS, dtype=jnp.int32)[:, None] == group_of[None, :]).astype(
        jnp.float32
    )
    gain_pair = jnp.stack([all_gain, all_tan])
    grid_pair = jnp.einsum("qpcd,dn->qpcn", gain_pair, dish_hot, precision=lax.Precision.HIGHEST)
    grid_gain = grid_pair[0].reshape(2, chans, ROWS, columns)
    grid_tan = grid_pair[1].reshape(2, chans, ROWS, columns)
    group_pair = jnp.stack([all_vis, all_gtan])
    canon_pair = jnp.einsum("qpcg,gk->qpck", group_pair, group_hot, precision=lax.Precision.HIGHEST)
    front = jnp.zeros((2, 2, chans, columns), jnp.float32)
    grid_both = jnp.concatenate([front, canon_pair], axis=3).reshape(2, 2, chans, ROWS, offsets)
    grid_vis = grid_both[0]
    grid_gtan = grid_both[1]
    first_row = block_list[:, 0]
    second_row = block_list[:, 1]
    row_gap = second_row - first_row
    row_ids = jnp.arange(ROWS, dtype=jnp.int32)[None, :]
    first_hot = (first_row[:, None] == row_ids).astype(jnp.float32)
    second_hot = (second_row[:, None] == row_ids).astype(jnp.float32)
    gap_hot = (row_gap[:, None] == row_ids).astype(jnp.float32)
    first_col = jnp.arange(columns)[:, None]
    second_col = jnp.arange(columns)[None, :]
    offset_table = (second_col - first_col + columns - 1).reshape(-1)
    member = (jnp.arange(offsets)[:, None] == offset_table[None, :]).astype(jnp.float32)
    upper = (second_col > first_col).reshape(-1)
    norm_factor = 1.0 / jnp.sqrt(jnp.float32(ROWS * columns))
    first_gain = select_rows(grid_gain, first_hot)[:, :, :, :, None]
    second_gain = select_rows(grid_gain, second_hot)[:, :, :, None, :]
    first_tan = select_rows(grid_tan, first_hot)[:, :, :, :, None]
    second_tan = select_rows(grid_tan, second_hot)[:, :, :, None, :]
    vis_rows = select_rows(grid_vis, gap_hot)
    tan_rows = select_rows(grid_gtan, gap_hot)
    shape_five = (2, chans, slots, columns, columns)
    toeplitz_vis = jnp.einsum(
        "pcbj,jn->pcbn", vis_rows, member, precision=lax.Precision.HIGHEST
    ).reshape(shape_five)
    toeplitz_tan = jnp.einsum(
        "pcbj,jn->pcbn", tan_rows, member, precision=lax.Precision.HIGHEST
    ).reshape(shape_five)
    valid = jnp.logical_or(row_gap[:, None] > 0, upper[None, :])
    weight_grid = (jnp.where(valid, weights.astype(jnp.float32), 0.0) * norm_factor).reshape(
        slots, columns, columns
    )
    pair_prod = times_complex(first_gain, conjugate(second_gain))
    gain_part = times_complex(first_tan, conjugate(second_gain)) + times_complex(
        first_gain, conjugate(second_tan)
    )
    model_tan = times_complex(gain_part, toeplitz_vis) + times_complex(pair_prod, toeplitz_tan)
    weighted = model_tan * weight_grid
    first_upd = jnp.sum(
        times_complex(weighted, times_complex(second_gain, conjugate(toeplitz_vis))), axis=4
    )
    second_upd = jnp.sum(
        times_complex(conjugate(weighted), times_complex(first_gain, toeplitz_vis)), axis=3
    )
    gain_grid = jnp.einsum("pcbk,br->pcrk", first_upd, first_hot, precision=lax.Precision.HIGHEST)
    gain_grid = gain_grid + jnp.einsum(
        "pcbk,br->pcrk", second_upd, second_hot, precision=lax.Precision.HIGHEST
    )
    group_field = times_complex(weighted, conjugate(pair_prod)).reshape(
        2, chans, slots, columns * columns
    )
    group_rows = jnp.einsum("pcbn,jn->pcbj", group_field, member, precision=lax.Precision.HIGHEST)
    group_grid = jnp.einsum("pcbj,br->pcrj", group_rows, gap_hot, precision=lax.Precision.HIGHEST)
    gain_flat = gain_grid.reshape(2, chans, DISHES)
    gain_full = jnp.einsum("pcn,dn->pcd", gain_flat, dish_hot, precision=lax.Precision.HIGHEST)
    canonical = group_grid.reshape(2, chans, ROWS * offsets)[:, :, columns:]
    group_full = jnp.einsum("pck,gk->pcg", canonical, group_hot, precision=lax.Precision.HIGHEST)
    gain_whole, group_whole = packed_total((gain_full, group_full), "bl")
    position = lax.axis_index("bl")
    gain_sum = lax.dynamic_slice_in_dim(gain_whole, position * dish_count, dish_count, 2)
    group_update = lax.dynamic_slice_in_dim(group_whole, position * group_count, group_count, 2)
    rimmed = extended(gain_tan, (("tf", 1),), 1)
    prior = 2.0 * gain_tan - rimmed[:, :-2] - rimmed[:, 2:]
    gain_update = gain_sum + prior_weight * prior
    return (gain_update, group_update)


def solution(mesh):
    placed = (
        P(None, "tf", "bl"),
        P(None, "tf", "bl"),
        P(None, "tf", "bl"),
        P(None, "tf", "bl"),
        P(),
        P(),
        P("bl", None),
        P("bl", None),
    )
    return jax.shard_map(
        local,
        mesh=mesh,
        in_specs=placed,
        out_specs=(P(None, "tf", "bl"), P(None, "tf", "bl")),
        check_vma=False,
    )
```

profile of v0, /device:TPU:24, one launch (start us, length us, event | category | flops | bytes accessed | tf_op | source)
XLA Modules:
  0.0 147.2 jit_solution(9524632239053969049)
XLA Ops:
  0.7 0.7 maximum_bitcast_fusion
  1.4 35.7 %all-gather = f32[16,64,8]{1,2,0:T(8,128)S(1)} all-gather(f32[1,64,8]{1,2,0:T(8,128)S(1)} %maximum_bitcast_fusion), channel_id=1, replica_groups=mesh['tf'=32,'bl'=16] {'bl'}, dimensions={0}, use_global_device_ids=true | all-gather | bytes 34816 | tf_op jit(solution)/shard_map/all_gather | solution.py:19
  37.3 2.2 %fusion.10 = f32[2,2,2,1024]{3,2,1,0:T(2,128)S(1)} fusion(s32[1024]{0:T(1024)} %param.12, f32[1,2,2,1024]{3,2,1,0:T(2,128)S(1)} %bitcast.166, f32[1,2,2,1024]{3,2,1,0:T(2,128)S(1)} %bitcast.165), kind=kOutput, calls=%fused_computation.10 | convolution fusion | flops 101720064 | bytes 69632 | tf_op jit(solution)/shard_map/qpcd,dn->qpcn/dot_general | solution.py:90
  39.6 0.2 convolution_bitcast_fusion.5
  39.9 0.6 slice_bitcast_fusion.3
  40.5 0.2 convolution_bitcast_fusion.4
  40.8 0.2 convolution_bitcast_fusion.6
  41.1 0.2 convolution_bitcast_fusion.3
  41.3 0.6 iota_compare_fusion.3
  41.9 0.5 compare_bitcast_fusion
  42.6 26.4 %all-gather.1 = f32[16,124,8]{1,2,0:T(8,128)S(1)} all-gather(f32[1,124,8]{1,2,0:T(8,128)S(1)} %maximum_bitcast_fusion.1), channel_id=1, replica_groups=mesh['tf'=32,'bl'=16] {'bl'}, dimensions={0}, use_global_device_ids=true | all-gather | bytes 67456 | tf_op jit(solution)/shard_map/all_gather | solution.py:19
  69.2 5.5 %fusion.2 = f32[2,2,2,1984]{3,2,1,0:T(2,128)S(1)} fusion(s32[1984]{0:T(1024)S(1)} %copy-done.17, f32[1,2,2,1984]{3,2,1,0:T(2,128)S(1)} %bitcast.163, f32[1,2,2,1984]{3,2,1,0:T(2,128)S(1)} %bitcast.162), kind=kOutput, calls=%fused_computation.3 | convolution fusion | flops 381832704 | bytes 134912 | tf_op jit(solution)/shard_map/qpcg,gk->qpck/dot_general | solution.py:94
  74.7 0.1 pad_slice_fusion
  74.8 0.1 squeeze.18
  75.1 0.2 convolution_bitcast_fusion
  75.3 0.4 fusion.28
  75.8 0.2 copy.127
  76.0 0.5 squeeze.19
  76.5 0.2 copy.128
  76.7 1.5 %squeeze.20 = f32[1,2,33,32,32]{4,3,1,2,0:T(8,128)} reshape(f32[1,2,33,1024]{3,1,2,0:T(2,128)S(1)} %copy.128) | data formatting | bytes 540672 | tf_op jit(solution)/shard_map/squeeze | solution.py:62
  78.2 0.7 copy.119
  78.9 0.7 copy.122
  79.6 0.7 copy.117
  80.3 0.7 copy.113
  81.0 0.7 copy.116
  81.7 0.7 copy.121
  82.4 0.7 copy.123
  83.1 0.1 squeeze.15
  83.3 0.2 convolution_bitcast_fusion.1
  83.5 0.4 fusion.30
  84.0 0.2 copy.125
  84.2 0.5 squeeze.16
  84.7 0.2 copy.126
  84.9 0.5 squeeze.17
  85.4 1.3 gt.27
  86.8 1.0 select_multiply_fusion
  87.8 1.0 mul.544
  88.8 0.9 copy.129
  89.7 3.2 %multiply_subtract_fusion.5 = (f32[1,2,33,32,32]{4,3,1,2,0:T(8,128)S(1)}, f32[1,2,33,32,32]{4,3,1,2,0:T(8,128)S(1)}, f32[1,2,33,32,32]{4,3,1,2,0:T(8,128)S(1)}, ...) fusion(f32[1,2,33,32,32]{4,3,1,2,0:T(8,128)} %squeeze.20, ...), kind=kLoop, calls=%fused_computation.40 | loop fusion | flops 1622016 | bytes 2230272 | tf_op jit(solution)/shard_map/sub | solution.py:62
  92.9 0.6 maximum_add_fusion
  93.5 0.5 multiply_subtract_fusion.7
  94.1 0.5 copy-done.1
  94.6 0.6 fusion.14
  95.2 2.6 %multiply_subtract_fusion = (f32[1,2,33,32,32]{4,3,1,2,0:T(8,128)}, f32[1,2,33,32,32]{4,3,1,2,0:T(8,128)S(1)}, f32[1,2,33,32,32]{4,3,1,2,0:T(8,128)S(1)}, f32[1,...) fusion(f32[2,2,33,32,32]{4,3,1,2,0:T(8,128)S(1)} %fusion.14, ...), kind=kLoop, calls=%fused_computation.30 | loop fusion | flops 2635776 | bytes 2745600 | tf_op jit(solution)/shard_map/sub | solution.py:62
  97.8 1.1 maximum_reduce_fusion
  98.9 0.2 fusion.36
  99.1 0.2 fusion.17
  99.3 0.1 reshape.350
  99.4 2.0 %fusion.18 = f32[2,8,2,128]{3,2,1,0:T(2,128)S(1)} fusion(f32[2,2,1024]{2,1,0:T(2,128)S(1)} %reshape.350, s32[1024]{0:T(1024)S(1)} %copy-done.19), kind=kOutput, calls=%fused_computation.28 | convolution fusion | flops 51380224 | bytes 36864 | tf_op jit(solution)/shard_map/pcn,dn->pcd/dot_general | solution.py:151
  101.4 0.6 stack.69
  102.1 0.6 stack.70
  102.8 0.5 fusion.22
  103.3 0.2 convolution_bitcast_fusion.2
  103.5 0.1 reshape.352
  103.6 7.5 %fusion.4 = f32[2,2,1984]{2,1,0:T(2,128)S(1)} fusion(s32[1984]{0:T(1024)S(1)} %copy-done.18, f32[2,2,2016]{2,1,0:T(2,128)S(1)} %reshape.352), kind=kOutput, calls=%fused_computation.4 | convolution fusion | flops 192876544 | bytes 71936 | tf_op jit(solution)/shard_map/pck,gk->pcg/dot_general | solution.py:153
  111.1 0.1 reshape.353
  111.2 1.3 broadcast_in_dim.6
  112.5 7.7 %all-to-all-start = ((f32[16,1,12032]{2,1,0:T(1,128)}), f32[16,1,12032]{2,1,0:T(1,128)S(1)}, u32[]{:S(2)}, u32[]{:S(2)}) async-start(f32[16,1,12032]{2,1,0:T(1,128)} %broadcast_in_dim.6), calls=%async_computation | async-start | bytes 1540096 | tf_op jit(solution)/shard_map/all_to_all | solution.py:31
  120.2 1.9 %collective-permute-start = (f32[2,1,64]{2,1,0:T(1,128)S(1)}, f32[2,1,64]{2,1,0:T(1,128)S(1)}, u32[]{:S(2)}, u32[]{:S(2)}) collective-permute-start(f32[2,1,64]{2,1,0:T(1,128)S(1)} %get-tuple-element.46), channel_id=1, source_target_pairs={{0,16},{16,32},{32,48},{48,64},{64,80},{80,96},{96,112},{112,128},... | collective-permute-start | bytes 1544 | tf_op jit(solution)/shard_map/ppermute | solution.py:54
  122.2 3.6 %collective-permute-start.1 = (f32[2,1,64]{2,1,0:T(1,128)S(1)}, f32[2,1,64]{2,1,0:T(1,128)S(1)}, u32[]{:S(2)}, u32[]{:S(2)}) collective-permute-start(f32[2,1,64]{2,1,0:T(1,128)S(1)} %get-tuple-element.47), channel_id=1, source_target_pairs={{16,0},{32,16},{48,32},{64,48},{80,64},{96,80},{112,96},{128,112},... | collective-permute-start | bytes 1544 | tf_op jit(solution)/shard_map/ppermute | solution.py:55
  125.8 19.4 %all-to-all-done = f32[16,1,12032]{2,1,0:T(1,128)S(1)} async-done(((f32[16,1,12032]{2,1,0:T(1,128)}), f32[16,1,12032]{2,1,0:T(1,128)S(1)}, u32[]{:S(2)}, u32[]{:S(2)}) %all-to-all-start) | async-done | bytes 770080 | tf_op jit(solution)/shard_map/all_to_all | solution.py:31
  145.2 0.5 reduce_sum.29
  145.8 0.7 constant_dynamic-slice_fusion
  146.5 0.7 fusion.69
  (74 shorter events, 1.2 us)
Async XLA Ops:
  0.6 38.9 %copy-start.16 = (s32[33,2]{0,1:T(2,128)S(1)}, s32[33,2]{0,1:T(2,128)}, u32[]{:S(2)}) copy-start(s32[33,2]{0,1:T(2,128)} %param.14) | copy-start | bytes 796
  37.2 5.3 %copy-start.14 = (f32[2,2,124]{2,1,0:T(2,128)S(1)}, f32[2,2,124]{2,1,0:T(2,128)}, u32[]{:S(2)}) copy-start(f32[2,2,124]{2,1,0:T(2,128)} %param.11) | copy-start | bytes 5956
  37.3 5.3 %copy-start.15 = (f32[2,2,124]{2,1,0:T(2,128)S(1)}, f32[2,2,124]{2,1,0:T(2,128)}, u32[]{:S(2)}) copy-start(f32[2,2,124]{2,1,0:T(2,128)} %param.10) | copy-start | bytes 5956
  39.4 29.8 %copy-start.17 = (s32[1984]{0:T(1024)S(1)}, s32[1984]{0:T(1024)}, u32[]{:S(2)}) copy-start(s32[1984]{0:T(1024)} %param.13) | copy-start | bytes 23812
  39.6 29.6 %copy-start.10 = (s32[33]{0:T(128)}, s32[33]{0:T(128)S(1)}, u32[]{:S(2)}) copy-start(s32[33]{0:T(128)S(1)} %get-tuple-element.50) | copy-start | bytes 400
  39.6 29.6 %copy-start.12 = (s32[33]{0:T(128)}, s32[33]{0:T(128)S(1)}, u32[]{:S(2)}) copy-start(s32[33]{0:T(128)S(1)} %get-tuple-element.48) | copy-start | bytes 400
  39.6 43.6 %copy-start.8 = (s32[33]{0:T(128)}, s32[33]{0:T(128)S(1)}, u32[]{:S(2)}) copy-start(s32[33]{0:T(128)S(1)} %get-tuple-element.49) | copy-start | bytes 400
  75.1 8.4 %copy-start.5 = (s32[1024]{0:T(1024)}, s32[1024]{0:T(1024)S(1)}, u32[]{:S(2)}) copy-start(s32[1024]{0:T(1024)S(1)} %sub.156) | copy-start | bytes 12292
  85.4 4.2 %copy-start.2 = (f32[2,33,32]{2,0,1:T(2,128)S(1)}, f32[2,33,32]{2,0,1:T(2,128)}, u32[]{:S(2)}) copy-start(f32[2,33,32]{2,0,1:T(2,128)} %copy.119) | copy-start | bytes 25348
  85.4 4.2 %copy-start.3 = (f32[2,33,32]{2,0,1:T(2,128)S(1)}, f32[2,33,32]{2,0,1:T(2,128)}, u32[]{:S(2)}) copy-start(f32[2,33,32]{2,0,1:T(2,128)} %copy.122) | copy-start | bytes 25348
  85.4 4.2 %copy-start.4 = (f32[2,33,32]{2,0,1:T(2,128)S(1)}, f32[2,33,32]{2,0,1:T(2,128)}, u32[]{:S(2)}) copy-start(f32[2,33,32]{2,0,1:T(2,128)} %copy.117) | copy-start | bytes 25348
  93.5 1.0 copy-start.1
  97.8 1.2 copy-start.13
  97.8 1.3 copy-start.11
  97.8 1.6 %copy-start.19 = (s32[1024]{0:T(1024)S(1)}, s32[1024]{0:T(1024)}, u32[]{:S(2)}) copy-start(s32[1024]{0:T(1024)} %param.12) | copy-start | bytes 12292
  98.9 2.5 %copy-start = (f32[1,2,33,32,32]{4,3,1,2,0:T(8,128)S(1)}, f32[1,2,33,32,32]{4,3,1,2,0:T(8,128)}, u32[]{:S(2)}) copy-start(f32[1,2,33,32,32]{4,3,1,2,0:T(8,128)} %get-tuple-element.10) | copy-start | bytes 811012
  102.1 0.7 copy-start.6
  102.1 1.2 copy-start.9
  102.7 0.9 copy-start.18
  111.2 9.0 %copy-start.7 = (f32[2,2,64]{2,1,0:T(2,128)S(1)}, f32[2,2,64]{2,1,0:T(2,128)}, u32[]{:S(2)}) copy-start(f32[2,2,64]{2,1,0:T(2,128)} %param.9) | copy-start | bytes 3076
  112.5 32.8 %all-to-all-start = ((f32[16,1,12032]{2,1,0:T(1,128)}), f32[16,1,12032]{2,1,0:T(1,128)S(1)}, u32[]{:S(2)}, u32[]{:S(2)}) async-start(f32[16,1,12032]{2,1,0:T(1,128)} %broadcast_in_dim.6), calls=%async_computation | async-start | bytes 1540096 | tf_op jit(solution)/shard_map/all_to_all | solution.py:31
  120.2 26.3 %collective-permute-start = (f32[2,1,64]{2,1,0:T(1,128)S(1)}, f32[2,1,64]{2,1,0:T(1,128)S(1)}, u32[]{:S(2)}, u32[]{:S(2)}) collective-permute-start(f32[2,1,64]{2,1,0:T(1,128)S(1)} %get-tuple-element.46), channel_id=1, source_target_pairs={{0,16},{16,32},{32,48},{48,64},{64,80},{80,96},{96,112},{112,128},... | collective-permute-start | bytes 1544 | tf_op jit(solution)/shard_map/ppermute | solution.py:54
  122.2 24.4 %collective-permute-start.1 = (f32[2,1,64]{2,1,0:T(1,128)S(1)}, f32[2,1,64]{2,1,0:T(1,128)S(1)}, u32[]{:S(2)}, u32[]{:S(2)}) collective-permute-start(f32[2,1,64]{2,1,0:T(1,128)S(1)} %get-tuple-element.47), channel_id=1, source_target_pairs={{16,0},{32,16},{48,32},{64,48},{80,64},{96,80},{112,96},{128,112},... | collective-permute-start | bytes 1544 | tf_op jit(solution)/shard_map/ppermute | solution.py:55
where the time goes:
time: 148 us; the launch traced here: 147 us
  blocking collectives  62.2 us (42%)
  matrix products  20.3 us (14%)
  waiting for transfers between devices  19.4 us (13%)
  local copies, waits for them, and re-layouts  18 us (12%)
  starting transfers between devices  13.3 us (9%)
  other arithmetic  12.7 us (9%)
    all_gather x2, blocking collectives, rows_first(): out = lax.all_gather(both, axis, axis=0, tiled=True)  62.2 us
    all_to_all x1, waiting for transfers between devices, from_everyone(): lax.all_to_all(jnp.broadcast_to(x[None], (peers, *x.shape)), axis, 0, 0,...  19.4 us
    all_to_all x1, starting transfers between devices, from_everyone(): lax.all_to_all(jnp.broadcast_to(x[None], (peers, *x.shape)), axis, 0, 0,...  7.71 us
    dot_general x1, matrix products, local(): jnp.einsum('pck,gk->pcg', canonical, group_hot, precision=lax.Precision.H...  7.48 us
    sub x3, other arithmetic, times_complex(): left[0] * right[0] - left[1] * right[1]  6.32 us
    dot_general x1, matrix products, local(): jnp.einsum('qpcg,gk->qpck', group_pair, group_hot, precision=lax.Precisio...  5.48 us
    ppermute x1, starting transfers between devices, extended(): after = lax.ppermute(first, axis, down)  3.64 us
  transfers between devices with their start and end apart: 3, of which 1 were waited for; matrix products, arithmetic and copies ran while one was open for 1% of the time, Pallas kernels for 0%

commit v1 on v0

v1 whole, which is shorter than its diff:
```python
import jax
import jax.numpy as jnp
from jax import lax
from jax.experimental import pallas as pl
from jax.experimental.pallas import tpu as pltpu
from jax.sharding import PartitionSpec as P

ROWS = 32
COLS = 32
DISHES = 1024
GROUPS = 1984
PRIOR_WEIGHT = 0.5

LANES = 128
PEERS = 16
DISH_PART = DISHES // PEERS
GROUP_PART = GROUPS // PEERS
CHANS = 2
SLOTS = 33
SLOT_GROUPS = 5
GATHER_WIDTH = 1536
SCATTER_WIDTH = 768

F32 = jnp.float32
I32 = jnp.int32


def iota(shape, dim):
    return lax.broadcasted_iota(I32, shape, dim)


def by_lane(x, idx):
    return jnp.take_along_axis(x, idx, axis=1)


def by_sublane(x, idx):
    return jnp.take_along_axis(x, idx, axis=0)


def div124(g):
    return ((g >> 2) * 16913) >> 19


def div63(n):
    return (n * 66577) >> 22


def spread(row, rows=8):
    return jnp.broadcast_to(row, (rows, LANES))


def prep_kernel(dish_ref, group_ref, blocks_ref, weights_ref, idx_ref, wts_ref):
    lane = iota((8, LANES), 1)
    sub = iota((8, LANES), 0)
    for half in range(2):
        dy = 16 * half + 2 * sub + (lane >> 6)
        wrapped = lane & 63
        dx = jnp.where(wrapped < 32, wrapped, wrapped - 64)
        k = dy * 63 + dx - 1
        ok = (k >= 0) & (wrapped != 32)
        chunk = k >> 7
        at = k & 127
        first = (16 * half * 63 - 32) // 128
        last = ((16 * half + 15) * 63 + 31) // 128
        found = jnp.zeros((8, LANES), I32)
        for c in range(max(first, 0), min(last, 15) + 1):
            row = spread(group_ref[c : c + 1, :])
            found = jnp.where(chunk == c, by_lane(row, at), found)
        zg = div124(found)
        idx_ref[8 * half : 8 * half + 8, :] = jnp.where(ok, zg, -1)
        idx_ref[16 + 8 * half : 24 + 8 * half, :] = found - 124 * zg
    peer = iota((PEERS, LANES), 0)
    low = iota((LANES, LANES), 0)
    nt = (((1,), (1,)), ((), ()))
    acc = jnp.zeros((2 * PEERS, LANES), F32)
    for c in range(8):
        ids = dish_ref[c : c + 1, :]
        hot = peer == (spread(ids, PEERS) >> 6)
        n_lane = iota((PEERS, LANES), 1)
        left = jnp.concatenate(
            [jnp.where(hot, float(c), 0.0), jnp.where(hot, n_lane, 0).astype(F32)], axis=0
        )
        right = (spread(ids, LANES) & 63) == (low & 63)
        acc = acc + lax.dot_general(
            left.astype(jnp.bfloat16),
            right.astype(F32).astype(jnp.bfloat16),
            nt,
            preferred_element_type=F32,
        )
    idx_ref[32:64, :] = (acc + 0.5).astype(I32)
    acc = jnp.zeros((2 * PEERS, LANES), F32)
    for c in range(16):
        ids = spread(group_ref[c : c + 1, :], PEERS)
        zone = div124(ids)
        n = LANES * c + iota((PEERS, LANES), 1)
        hot = (peer == zone) & (n < GROUPS)
        dy = div63(n + 32)
        dx = n + 32 - 63 * dy - 31
        table_row = dy >> 1
        table_lane = 64 * (dy & 1) + (dx & 63)
        left = jnp.concatenate(
            [jnp.where(hot, table_row, 0), jnp.where(hot, table_lane, 0)], axis=0
        ).astype(F32)
        rest = (ids - 124 * zone)[0:1, :]
        right = spread(rest, LANES) == low
        acc = acc + lax.dot_general(
            left.astype(jnp.bfloat16),
            right.astype(F32).astype(jnp.bfloat16),
            nt,
            preferred_element_type=F32,
        )
    idx_ref[64:96, :] = (acc + 0.5).astype(I32)
    for g in range(SLOT_GROUPS):
        if g < 4:
            pairs = blocks_ref[8 * g : 8 * g + 8, :]
            gap = jnp.broadcast_to(pairs[:, 1:2] - pairs[:, 0:1], (8, LANES))
        else:
            pairs = blocks_ref[32:33, :]
            gap = jnp.broadcast_to(pairs[:, 1:2] - pairs[:, 0:1], (8, LANES))
        for j in range(8):
            cols = slice(LANES * j, LANES * j + LANES)
            first_col = 4 * j + (lane >> 5)
            second_col = lane & 31
            ok = (gap > 0) | (second_col > first_col)
            if g < 4:
                w = weights_ref[8 * g : 8 * g + 8, cols]
            else:
                w = spread(weights_ref[32:33, cols])
                ok = ok & (sub == 0)
            wts_ref[8 * g : 8 * g + 8, cols] = jnp.where(ok, w.astype(F32), 0.0) * (1.0 / 32.0)


def main_kernel(recv_ref, dish_ref, blocks_ref, idx_ref, wts_ref, out_ref, gtab, ytab, ff, ss, gg, gout, yout):
    lane = iota((8, LANES), 1)
    sub = iota((8, LANES), 0)
    quad = lane >> 5
    col = lane & 31
    dish = dish_ref[...]
    zone = dish >> 6
    at = dish & 63
    for b in range(4):
        res = [jnp.zeros((8, LANES), F32), jnp.zeros((8, LANES), F32)]
        for z in range(PEERS):
            row = spread(recv_ref[z, :, LANES * b : LANES * b + LANES])
            hit = zone == z
            for c in range(CHANS):
                res[c] = jnp.where(hit, by_lane(row, at + 64 * c), res[c])
        for c in range(CHANS):
            gtab[2 * b + c] = res[c]
    for b in range(8):
        res = [jnp.zeros((8, LANES), F32), jnp.zeros((8, LANES), F32)]
        for z in range(PEERS):
            row = spread(recv_ref[z, :, 512 + LANES * b : 512 + LANES * b + LANES])
            for h in range(2):
                hit = idx_ref[8 * h : 8 * h + 8, :] == z
                res[h] = jnp.where(hit, by_lane(row, idx_ref[16 + 8 * h : 24 + 8 * h, :]), res[h])
        ytab[b, 0:8, :] = res[0]
        ytab[b, 8:16, :] = res[1]
    half_lo = (lane & 16) == 0
    quarter_lo = (lane & 8) == 0
    eighth_lo = (lane & 4) == 0
    sorted_idx = 32 * (col & 3) + 16 * ((col >> 2) & 1) + 8 * ((col >> 3) & 1) + 4 * ((col >> 4) & 1)

    def merge(a, b, low, bit):
        return jnp.where(low, a, b) + by_lane(jnp.where(low, b, a), lane ^ bit)

    for g in range(SLOT_GROUPS):
        if g < 4:
            pairs = blocks_ref[8 * g : 8 * g + 8, :]
        else:
            pairs = blocks_ref[32:33, :]
        r1 = jnp.broadcast_to(pairs[:, 0:1], (8, LANES))
        r2 = jnp.broadcast_to(pairs[:, 1:2], (8, LANES))
        dy = r2 - r1
        slots = slice(8 * g, 8 * g + 8)
        base1 = 32 * (r1 & 3) + quad
        base2 = 32 * (r2 & 3) + col
        basey = 64 * (dy & 1)
        for c in range(CHANS):
            src_a = [by_sublane(gtab[2 * b + c], r1 >> 2) for b in range(4)]
            gb = [by_lane(by_sublane(gtab[2 * b + c], r2 >> 2), base2) for b in range(4)]
            src_y = []
            for b in range(4):
                low = by_sublane(ytab[2 * b + c, 0:8, :], (dy >> 1) & 7)
                high = by_sublane(ytab[2 * b + c, 8:16, :], (dy >> 1) & 7)
                src_y.append(jnp.where(dy < 16, low, high))
            gbr, gbi, dbr, dbi = gb
            f_re, f_im = [], []
            s_re = s_im = pos_re = pos_im = neg_re = neg_im = None
            for j in range(8):
                idx_a = base1 + 4 * j
                ga_r, ga_i, da_r, da_i = [by_lane(v, idx_a) for v in src_a]
                first_col = 4 * j + quad
                idx_y = basey + ((col - first_col) & 63)
                y_r, y_i, t_r, t_i = [by_lane(v, idx_y) for v in src_y]
                w = wts_ref[slots, LANES * j : LANES * j + LANES]
                p_r = ga_r * gbr + ga_i * gbi
                p_i = ga_i * gbr - ga_r * gbi
                q_r = (da_r * gbr + da_i * gbi) + (ga_r * dbr + ga_i * dbi)
                q_i = (da_i * gbr - da_r * gbi) + (ga_i * dbr - ga_r * dbi)
                u_r = w * ((q_r * y_r - q_i * y_i) + (p_r * t_r - p_i * t_i))
                u_i = w * ((q_r * y_i + q_i * y_r) + (p_r * t_i + p_i * t_r))
                v_r = u_r * y_r + u_i * y_i
                v_i = u_i * y_r - u_r * y_i
                f_re.append(v_r * gbr - v_i * gbi)
                f_im.append(v_r * gbi + v_i * gbr)
                a_r = v_r * ga_r + v_i * ga_i
                a_i = v_r * ga_i - v_i * ga_r
                d_r = u_r * p_r + u_i * p_i
                d_i = u_i * p_r - u_r * p_i
                shift = (lane & 96) | ((col + first_col) & 31)
                straight = col + first_col < 32
                d_r = by_lane(d_r, shift)
                d_i = by_lane(d_i, shift)
                pr = jnp.where(straight, d_r, 0.0)
                pi = jnp.where(straight, d_i, 0.0)
                nr = jnp.where(straight, 0.0, d_r)
                ni = jnp.where(straight, 0.0, d_i)
                if j == 0:
                    s_re, s_im, pos_re, pos_im, neg_re, neg_im = a_r, a_i, pr, pi, nr, ni
                else:
                    s_re = s_re + a_r
                    s_im = s_im + a_i
                    pos_re = pos_re + pr
                    pos_im = pos_im + pi
                    neg_re = neg_re + nr
                    neg_im = neg_im + ni
            here1 = (r1 & 3) == quad
            here2 = (r2 & 3) == quad
            herey = (dy & 1) == (lane >> 6)
            for p, vals in enumerate((f_re, f_im)):
                lv = [merge(vals[2 * k], vals[2 * k + 1], half_lo, 16) for k in range(4)]
                lv = [merge(lv[2 * k], lv[2 * k + 1], quarter_lo, 8) for k in range(2)]
                one = merge(lv[0], lv[1], eighth_lo, 4)
                one = one + by_lane(one, lane ^ 2)
                one = one + by_lane(one, lane ^ 1)
                one = by_lane(one, sorted_idx)
                ff[slots, LANES * (2 * p + c) : LANES * (2 * p + c + 1)] = jnp.where(here1, one, 0.0)
            for p, one in enumerate((s_re, s_im)):
                one = one + by_lane(one, lane ^ 32)
                one = one + by_lane(one, lane ^ 64)
                ff[slice(40 + 8 * g, 48 + 8 * g), LANES * (2 * p + c) : LANES * (2 * p + c + 1)] = jnp.where(
                    here2, one, 0.0
                )
            for p, (a, b) in enumerate(((pos_re, neg_re), (pos_im, neg_im))):
                low = (lane & 32) == 0
                one = merge(a, b, low, 32)
                one = one + by_lane(one, lane ^ 64)
                gg[slots, LANES * (2 * p + c) : LANES * (2 * p + c + 1)] = jnp.where(herey, one, 0.0)
        ss[slots, :] = ((r1 >> 2) == lane).astype(F32)
        ss[slice(40 + 8 * g, 48 + 8 * g), :] = ((r2 >> 2) == lane).astype(F32)
        ss[slice(80 + 8 * g, 88 + 8 * g), :] = ((dy >> 1) == lane).astype(F32)
    tn = (((0,), (0,)), ((), ()))
    gout[...] = lax.dot_general(
        ss[0:80, :], ff[...], tn, precision=lax.Precision.HIGHEST, preferred_element_type=F32
    )[0:8, :]
    yout[...] = lax.dot_general(
        ss[80:120, :], gg[...], tn, precision=lax.Precision.HIGHEST, preferred_element_type=F32
    )[0:16, :]
    for h in range(2):
        rows = slice(8 * h, 8 * h + 8)
        at_row = idx_ref[32 + 8 * h : 40 + 8 * h, :]
        at_lane = idx_ref[48 + 8 * h : 56 + 8 * h, :]
        for p in range(2):
            res = jnp.zeros((8, LANES), F32)
            for c in range(CHANS):
                mine = (lane >> 6) == c
                for k in range(8):
                    row = spread(gout[k : k + 1, LANES * (2 * p + c) : LANES * (2 * p + c + 1)])
                    res = jnp.where(mine & (at_row == k), by_lane(row, at_lane), res)
            out_ref[rows, 0, 512 + LANES * p : 512 + LANES * (p + 1)] = res
        at_row = idx_ref[64 + 8 * h : 72 + 8 * h, :]
        at_lane = idx_ref[80 + 8 * h : 88 + 8 * h, :]
        for q in range(4):
            res = jnp.zeros((8, LANES), F32)
            for k in range(16):
                row = spread(yout[k : k + 1, LANES * q : LANES * (q + 1)])
                res = jnp.where(at_row == k, by_lane(row, at_lane), res)
            out_ref[rows, 0, LANES * q : LANES * (q + 1)] = res


def final_kernel(recv_ref, tan_ref, before_ref, after_ref, gain_ref, group_ref):
    for p in range(2):
        before = before_ref[p]
        after = after_ref[p]
        t0 = tan_ref[p, 0:1, :]
        t1 = tan_ref[p, 1:2, :]
        prior = [2.0 * t0 - before - t1, 2.0 * t1 - t0 - after]
        total = recv_ref[0, :, 512 + LANES * p : 512 + LANES * (p + 1)]
        for z in range(1, PEERS):
            total = total + recv_ref[z, :, 512 + LANES * p : 512 + LANES * (p + 1)]
        for c in range(CHANS):
            gain_ref[p, c : c + 1, :] = total[:, 64 * c : 64 * c + 64] + PRIOR_WEIGHT * prior[c]
            q = 2 * p + c
            sums = recv_ref[0, :, LANES * q : LANES * (q + 1)]
            for z in range(1, PEERS):
                sums = sums + recv_ref[z, :, LANES * q : LANES * (q + 1)]
            group_ref[p, c : c + 1, :] = sums[:, 0:GROUP_PART]


def local(gains, gain_tan, group_vis, group_tan, dish_of, group_of, block_list, weights):
    shape = jax.ShapeDtypeStruct
    pad = ((0, 0), (0, 0), (0, LANES - GROUP_PART))
    message = jnp.concatenate(
        [
            gains.reshape(-1),
            gain_tan.reshape(-1),
            jnp.pad(group_vis, pad).reshape(-1),
            jnp.pad(group_tan, pad).reshape(-1),
        ]
    )
    sent = jnp.broadcast_to(message[None, None], (PEERS, 1, GATHER_WIDTH))
    gathered = lax.all_to_all(sent, "bl", 0, 0, tiled=True)
    peers = lax.axis_size("tf")
    up = [(i, i + 1) for i in range(peers - 1)]
    down = [(j, i) for i, j in up]
    before = lax.ppermute(gain_tan[:, 1:2], "tf", up)
    after = lax.ppermute(gain_tan[:, 0:1], "tf", down)
    dish_table = dish_of.reshape(8, LANES)
    group_table = jnp.pad(group_of, (0, 16 * LANES - GROUPS)).reshape(16, LANES)
    idx, wts = pl.pallas_call(
        prep_kernel,
        out_shape=(shape((96, LANES), I32), shape((8 * SLOT_GROUPS, 1024), F32)),
        name="prep",
    )(dish_table, group_table, block_list, weights)
    partial = pl.pallas_call(
        main_kernel,
        out_shape=shape((PEERS, 1, SCATTER_WIDTH), F32),
        scratch_shapes=[
            pltpu.VMEM((8, 8, LANES), F32),
            pltpu.VMEM((8, 16, LANES), F32),
            pltpu.VMEM((80, 4 * LANES), F32),
            pltpu.VMEM((120, LANES), F32),
            pltpu.VMEM((40, 4 * LANES), F32),
            pltpu.VMEM((8, 4 * LANES), F32),
            pltpu.VMEM((16, 4 * LANES), F32),
        ],
        name="main",
    )(gathered, dish_table, block_list, idx, wts)
    parts = lax.all_to_all(partial, "bl", 0, 0, tiled=True)
    return pl.pallas_call(
        final_kernel,
        out_shape=(shape((2, CHANS, DISH_PART), F32), shape((2, CHANS, GROUP_PART), F32)),
        name="finish",
    )(parts, gain_tan, before, after)


def solution(mesh):
    placed = (
        P(None, "tf", "bl"),
        P(None, "tf", "bl"),
        P(None, "tf", "bl"),
        P(None, "tf", "bl"),
        P(),
        P(),
        P("bl", None),
        P("bl", None),
    )
    return jax.shard_map(
        local,
        mesh=mesh,
        in_specs=placed,
        out_specs=(P(None, "tf", "bl"), P(None, "tf", "bl")),
        check_vma=False,
    )
```

time: 148 us -> 68.6 us (0.46)
  blocking collectives: 62.2 us -> 0 us
  Pallas kernels: 0 us -> 20.4 us
  matrix products: 20.3 us -> 0 us
  other arithmetic: 12.7 us -> 0.01 us
  local copies, waits for them, and re-layouts: 18 us -> 5.37 us
  starting transfers between devices: 13.3 us -> 24.4 us
  waiting for transfers between devices: 19.4 us -> 17.3 us
    all_gather x2 -> x0, blocking collectives: 62.2 us -> none  [rows_first(): out = lax.all_gather(both, axis, axis=0, tiled=True)]
    pallas_call x0 -> x3, Pallas kernels: none -> 20.4 us  [the longest x1 16.7 us: local(): pl.pallas_call(main_kernel, out_shape=shape((PEERS, 1, SCATTER_WIDTH), F3...]
    dot_general x16 -> x0, matrix products: 20.3 us -> none  [the longest x1 7.48 us: local(): jnp.einsum('pck,gk->pcg', canonical, group_hot, precision=lax.Precision.H...]
    all_to_all x1 -> x2, starting transfers between devices: 7.71 us -> 18.8 us  [the longest x1 15.3 us: local(): gathered = lax.all_to_all(sent, 'bl', 0, 0, tiled=True)]
    sub x4 -> x0, other arithmetic: 6.33 us -> none  [the longest x3 6.32 us: times_complex(): left[0] * right[0] - left[1] * right[1]]
    squeeze x8 -> x0, local copies, waits for them, and re-layouts: 4.65 us -> none  [the longest x2 1.97 us: times_complex(): right[1]]
    mul x9 -> x0, local copies, waits for them, and re-layouts: 4.59 us -> none  [the longest x6 2.21 us: times_complex(): left[0] * right[0] - left[1] * right[1]]
    all_to_all x1 -> x2, waiting for transfers between devices: 19.4 us -> 16 us  [the longest x1 10.2 us: local(): gathered = lax.all_to_all(sent, 'bl', 0, 0, tiled=True)]
  transfers between devices with their start and end apart: 3 -> 4, of which waited for: 1 -> 3; matrix products, arithmetic and copies ran while one was open for 1% -> 2% of each run, Pallas kernels for 0% -> 3%
where the time goes in v1:
time: 68.6 us; the launch traced here: 68.1 us
  starting transfers between devices  24.4 us (36%)
  Pallas kernels  20.4 us (30%)
  waiting for transfers between devices  17.3 us (25%)
  local copies, waits for them, and re-layouts  5.37 us (8%)
  between operations  0.72 us (1%)
    pallas_call x1, Pallas kernels, local(): pl.pallas_call(main_kernel, out_shape=shape((PEERS, 1, SCATTER_WIDTH), F3...  16.7 us
    all_to_all x1, starting transfers between devices, local(): gathered = lax.all_to_all(sent, 'bl', 0, 0, tiled=True)  15.3 us
    all_to_all x1, waiting for transfers between devices, local(): gathered = lax.all_to_all(sent, 'bl', 0, 0, tiled=True)  10.2 us
    all_to_all x1, waiting for transfers between devices, local(): parts = lax.all_to_all(partial, 'bl', 0, 0, tiled=True)  5.79 us
    ppermute x1, starting transfers between devices, local(): after = lax.ppermute(gain_tan[:, 0:1], 'tf', down)  3.64 us
    all_to_all x1, starting transfers between devices, local(): parts = lax.all_to_all(partial, 'bl', 0, 0, tiled=True)  3.5 us
    unnamed x19, local copies, waits for them, and re-layouts  3.22 us
    pallas_call x1, Pallas kernels, local(): pl.pallas_call(prep_kernel, out_shape=(shape((96, LANES), I32), shape((8...  2.12 us
  transfers between devices with their start and end apart: 4, of which 3 were waited for; matrix products, arithmetic and copies ran while one was open for 2% of the time, Pallas kernels for 3%

profile of v1, /device:TPU:24, one launch (start us, length us, event | category | flops | bytes accessed | tf_op | source)
XLA Modules:
  0.0 68.1 jit_solution(12247704875703848777)
XLA Ops:
  0.6 0.0 copy-start.5
  0.6 0.7 %pad.12 = f32[2,2,128]{2,1,0:T(2,128)S(1)} pad(f32[2,2,124]{2,1,0:T(2,128)} %param.11, f32[]{:T(128)} %constant.2.clone.1), padding=0_0x0_0x0_4 | pad | bytes 4036 | tf_op jit(solution)/shard_map/jit(_pad)/pad | solution.py:309
  1.3 0.0 copy-done.5
  1.3 0.0 copy-start.2
  1.3 0.7 copy-done.2
  2.0 0.0 copy-start.4
  2.0 0.1 reshape.26
  2.1 0.6 copy-done.4
  2.7 0.1 reshape.25
  2.8 0.7 %broadcast_in_dim.2 = f32[16,1,1536]{2,1,0:T(1,128)} broadcast(f32[1536]{0:T(1024)S(1)} %pad_maximum_fusion), dimensions={2} | broadcast | bytes 104448 | tf_op jit(solution)/shard_map/broadcast_in_dim | solution.py:312
  3.5 0.0 copy-start.6
  3.5 15.3 %all-to-all-start = ((f32[16,1,1536]{2,1,0:T(1,128)}), f32[16,1,1536]{2,1,0:T(1,128)S(1)}, u32[]{:S(2)}, u32[]{:S(2)}) async-start(f32[16,1,1536]{2,1,0:T(1,128)} %broadcast_in_dim.2), calls=%async_computation | async-start | bytes 196608 | tf_op jit(solution)/shard_map/all_to_all | solution.py:313
  18.8 0.0 copy-done.6
  18.8 0.0 copy-start.3
  18.8 0.7 %copy.11.blocks_ref = s32[33,2]{1,0:T(8,128)} copy(s32[33,2]{0,1:T(2,128)S(1)} %copy-done.6) | data formatting | bytes 528 | tf_op args[6]
  19.5 0.0 copy-done.3
  19.5 0.6 pad_bitcast_fusion.group_ref
  20.1 2.1 %prep.1 = (s32[96,128]{1,0:T(8,128)}, f32[40,1024]{1,0:T(8,128)}) custom-call(s32[8,128]{1,0:T(8,128)} %bitcast.5, s32[16,128]{1,0:T(8,128)} %pad_bitcast_fusion.group_ref, s32[33,2]{1,0:T(8,128)} %copy.11.blocks_ref, s32[33,1024]{1,0:T(8,128)} %weights_ref.1), custom_call_target="tpu_custom_call" | custom-call | tf_op jit(solution)/shard_map/prep/pallas_call | solution.py:321
  22.2 10.2 %all-to-all-done.recv_ref = f32[16,1,1536]{2,1,0:T(1,128)S(1)} async-done(((f32[16,1,1536]{2,1,0:T(1,128)}), f32[16,1,1536]{2,1,0:T(1,128)S(1)}, u32[]{:S(2)}, u32[]{:S(2)}) %all-to-all-start) | async-done | bytes 98336 | tf_op jit(solution)/shard_map/all_to_all | solution.py:313
  32.5 0.0 copy-start
  32.5 0.6 copy-done
  33.1 16.7 %main.1 = f32[16,1,768]{2,1,0:T(1,128)} custom-call(f32[16,1,1536]{2,1,0:T(1,128)} %copy-done, s32[8,128]{1,0:T(8,128)} %bitcast.6, s32[33,2]{1,0:T(8,128)} %copy.11.blocks_ref, s32[96,128]{1,0:T(8,128)} %get-tuple-element.4.idx_ref, f32[40,1024]{1,0:T(8,128)} %get-tuple-element.5.wts_ref), custom_call_target="tpu_custom_call" | custom-call | tf_op jit(solution)/shard_map/main/pallas_call | solution.py:326
  49.8 3.5 %all-to-all-start.1 = ((f32[16,1,768]{2,1,0:T(1,128)}), f32[16,1,768]{2,1,0:T(1,128)S(1)}, u32[]{:S(2)}, u32[]{:S(2)}) async-start(f32[16,1,768]{2,1,0:T(1,128)} %main.1), calls=%async_computation.1 | async-start | bytes 98304 | tf_op jit(solution)/shard_map/all_to_all | solution.py:340
  53.3 1.9 %collective-permute-start = (f32[2,1,64]{2,1,0:T(1,128)S(1)}, f32[2,1,64]{2,1,0:T(1,128)S(1)}, u32[]{:S(2)}, u32[]{:S(2)}) collective-permute-start(f32[2,1,64]{2,1,0:T(1,128)S(1)} %get-tuple-element.7), channel_id=1, source_target_pairs={{0,16},{16,32},{32,48},{48,64},{64,80},{80,96},{96,112},{112,128},... | collective-permute-start | bytes 1544 | tf_op jit(solution)/shard_map/ppermute | solution.py:317
  55.3 3.6 %collective-permute-start.1 = (f32[2,1,64]{2,1,0:T(1,128)S(1)}, f32[2,1,64]{2,1,0:T(1,128)S(1)}, u32[]{:S(2)}, u32[]{:S(2)}) collective-permute-start(f32[2,1,64]{2,1,0:T(1,128)S(1)} %get-tuple-element.6), channel_id=1, source_target_pairs={{16,0},{32,16},{48,32},{64,48},{80,64},{96,80},{112,96},{128,112},... | collective-permute-start | bytes 1544 | tf_op jit(solution)/shard_map/ppermute | solution.py:318
  58.9 0.0 collective-permute-done.before_ref
  58.9 0.0 copy-start.7
  58.9 1.3 %collective-permute-done.1.after_ref = f32[2,1,64]{2,1,0:T(1,128)S(1)} collective-permute-done((f32[2,1,64]{2,1,0:T(1,128)S(1)}, f32[2,1,64]{2,1,0:T(1,128)S(1)}, u32[]{:S(2)}, u32[]{:S(2)}) %collective-permute-start.1) | collective-permute-done | bytes 544 | tf_op jit(solution)/shard_map/ppermute | solution.py:318
  60.2 0.0 copy-start.8
  60.2 5.8 %all-to-all-done.1.recv_ref = f32[16,1,768]{2,1,0:T(1,128)S(1)} async-done(((f32[16,1,768]{2,1,0:T(1,128)}), f32[16,1,768]{2,1,0:T(1,128)S(1)}, u32[]{:S(2)}, u32[]{:S(2)}) %all-to-all-start.1) | async-done | bytes 49184 | tf_op jit(solution)/shard_map/all_to_all | solution.py:340
  66.0 0.0 copy-done.7
  66.0 0.0 copy-done.8
  66.0 0.0 copy-start.1
  66.0 0.6 copy-done.1
  66.6 1.5 %finish.1 = (f32[2,2,64]{2,1,0:T(2,128)}, f32[2,2,124]{2,1,0:T(2,128)}) custom-call(f32[16,1,768]{2,1,0:T(1,128)} %copy-done.1, f32[2,2,64]{2,1,0:T(2,128)} %tan_ref.1, f32[2,1,64]{2,1,0:T(1,128)} %copy-done.7, f32[2,1,64]{2,1,0:T(1,128)} %copy-done.8), custom_call_target="tpu_custom_call" | custom-call | tf_op jit(solution)/shard_map/finish/pallas_call | solution.py:341
  (3 shorter events, 0.0 us)
Async XLA Ops:
  0.6 0.7 %copy-start.5 = (f32[2,2,124]{2,1,0:T(2,128)S(1)}, f32[2,2,124]{2,1,0:T(2,128)}, u32[]{:S(2)}) copy-start(f32[2,2,124]{2,1,0:T(2,128)} %param.10) | copy-start | bytes 5956
  1.3 0.7 %copy-start.2 = (f32[2,2,64]{2,1,0:T(2,128)S(1)}, f32[2,2,64]{2,1,0:T(2,128)}, u32[]{:S(2)}) copy-start(f32[2,2,64]{2,1,0:T(2,128)} %tan_ref.1) | copy-start | bytes 3076
  2.0 0.7 %copy-start.4 = (f32[2,2,64]{2,1,0:T(2,128)S(1)}, f32[2,2,64]{2,1,0:T(2,128)}, u32[]{:S(2)}) copy-start(f32[2,2,64]{2,1,0:T(2,128)} %param.8) | copy-start | bytes 3076
  3.5 15.3 %copy-start.6 = (s32[33,2]{0,1:T(2,128)S(1)}, s32[33,2]{0,1:T(2,128)}, u32[]{:S(2)}) copy-start(s32[33,2]{0,1:T(2,128)} %param.14) | copy-start | bytes 796
  3.5 29.0 %all-to-all-start = ((f32[16,1,1536]{2,1,0:T(1,128)}), f32[16,1,1536]{2,1,0:T(1,128)S(1)}, u32[]{:S(2)}, u32[]{:S(2)}) async-start(f32[16,1,1536]{2,1,0:T(1,128)} %broadcast_in_dim.2), calls=%async_computation | async-start | bytes 196608 | tf_op jit(solution)/shard_map/all_to_all | solution.py:313
  18.8 0.7 %copy-start.3 = (s32[1984]{0:T(1024)S(1)}, s32[1984]{0:T(1024)}, u32[]{:S(2)}) copy-start(s32[1984]{0:T(1024)} %param.13) | copy-start | bytes 23812
  32.5 0.6 copy-start
  49.8 16.2 %all-to-all-start.1 = ((f32[16,1,768]{2,1,0:T(1,128)}), f32[16,1,768]{2,1,0:T(1,128)S(1)}, u32[]{:S(2)}, u32[]{:S(2)}) async-start(f32[16,1,768]{2,1,0:T(1,128)} %main.1), calls=%async_computation.1 | async-start | bytes 98304 | tf_op jit(solution)/shard_map/all_to_all | solution.py:340
  53.3 5.6 %collective-permute-start = (f32[2,1,64]{2,1,0:T(1,128)S(1)}, f32[2,1,64]{2,1,0:T(1,128)S(1)}, u32[]{:S(2)}, u32[]{:S(2)}) collective-permute-start(f32[2,1,64]{2,1,0:T(1,128)S(1)} %get-tuple-element.7), channel_id=1, source_target_pairs={{0,16},{16,32},{32,48},{48,64},{64,80},{80,96},{96,112},{112,128},... | collective-permute-start | bytes 1544 | tf_op jit(solution)/shard_map/ppermute | solution.py:317
  55.3 4.9 %collective-permute-start.1 = (f32[2,1,64]{2,1,0:T(1,128)S(1)}, f32[2,1,64]{2,1,0:T(1,128)S(1)}, u32[]{:S(2)}, u32[]{:S(2)}) collective-permute-start(f32[2,1,64]{2,1,0:T(1,128)S(1)} %get-tuple-element.6), channel_id=1, source_target_pairs={{16,0},{32,16},{48,32},{64,48},{80,64},{96,80},{112,96},{128,112},... | collective-permute-start | bytes 1544 | tf_op jit(solution)/shard_map/ppermute | solution.py:318
  58.9 7.1 %copy-start.7 = (f32[2,1,64]{2,1,0:T(1,128)}, f32[2,1,64]{2,1,0:T(1,128)S(1)}, u32[]{:S(2)}) copy-start(f32[2,1,64]{2,1,0:T(1,128)S(1)} %collective-permute-done.before_ref) | copy-start | bytes 1540
  60.2 5.8 %copy-start.8 = (f32[2,1,64]{2,1,0:T(1,128)}, f32[2,1,64]{2,1,0:T(1,128)S(1)}, u32[]{:S(2)}) copy-start(f32[2,1,64]{2,1,0:T(1,128)S(1)} %collective-permute-done.1.after_ref) | copy-start | bytes 1540
  66.0 0.6 copy-start.1

commit v2 on v1

v2 whole, which is shorter than its diff:
```python
import jax
import jax.numpy as jnp
from jax import lax
from jax.experimental import pallas as pl
from jax.experimental.pallas import tpu as pltpu
from jax.sharding import PartitionSpec as P

ROWS = 32
COLS = 32
DISHES = 1024
GROUPS = 1984
PRIOR_WEIGHT = 0.5

LANES = 128
PEERS = 16
DISH_PART = DISHES // PEERS
GROUP_PART = GROUPS // PEERS
CHANS = 2
SLOTS = 33
SLOT_GROUPS = 5
GATHER_WIDTH = 1536
SCATTER_WIDTH = 768
PARTS = 3

F32 = jnp.float32
I32 = jnp.int32


def iota(shape, dim):
    return lax.broadcasted_iota(I32, shape, dim)


def by_lane(x, idx):
    return jnp.take_along_axis(x, idx, axis=1)


def by_sublane(x, idx):
    return jnp.take_along_axis(x, idx, axis=0)


def div124(g):
    return ((g >> 2) * 16913) >> 19


def div63(n):
    return (n * 66577) >> 22


def spread(row, rows=8):
    return jnp.broadcast_to(row, (rows, LANES))

BF16 = jnp.bfloat16
ROWS_ALL = 8 * 8 * SLOT_GROUPS


def split3(x):
    hi = x.astype(BF16).astype(F32)
    rest = x - hi
    mid = rest.astype(BF16).astype(F32)
    return hi, mid, rest - mid


def pack_kernel(gain_ref, tan_ref, vis_ref, gtan_ref, out_ref):
    for k, ref in enumerate((gain_ref, tan_ref)):
        for p in range(2):
            row = jnp.concatenate([ref[p, 0:1, :], ref[p, 1:2, :]], axis=1)
            at = LANES * (2 * k + p)
            out_ref[:, 0, at : at + LANES] = spread(row, PEERS)
    fill = jnp.zeros((1, LANES - GROUP_PART), F32)
    for k, ref in enumerate((vis_ref, gtan_ref)):
        for p in range(2):
            for c in range(CHANS):
                row = jnp.concatenate([ref[p, c : c + 1, :], fill], axis=1)
                at = 512 + LANES * (4 * k + 2 * p + c)
                out_ref[:, 0, at : at + LANES] = spread(row, PEERS)


def prep_kernel(
    dish_ref, group_ref, blocks_ref, turned_ref, weights_ref,
    idx_ref, wts_ref, hot_ref, e1_ref, e2_ref, ey_ref, s1_ref, sd_ref,
):
    lane = iota((8, LANES), 1)
    sub = iota((8, LANES), 0)
    for half in range(2):
        dy = 16 * half + 2 * sub + (lane >> 6)
        wrapped = lane & 63
        dx = jnp.where(wrapped < 32, wrapped, wrapped - 64)
        k = dy * 63 + dx - 1
        ok = (k >= 0) & (wrapped != 32)
        chunk = k >> 7
        at = k & 127
        first = (16 * half * 63 - 32) // 128
        last = ((16 * half + 15) * 63 + 31) // 128
        found = jnp.zeros((8, LANES), I32)
        for c in range(max(first, 0), min(last, 15) + 1):
            row = spread(group_ref[c : c + 1, :])
            found = jnp.where(chunk == c, by_lane(row, at), found)
        zg = div124(found)
        idx_ref[8 * half : 8 * half + 8, :] = jnp.where(ok, zg, -1)
        idx_ref[16 + 8 * half : 24 + 8 * half, :] = found - 124 * zg
    peer = iota((PEERS, LANES), 0)
    low = iota((LANES, LANES), 0)
    nt = (((1,), (1,)), ((), ()))
    acc = jnp.zeros((2 * PEERS, LANES), F32)
    for c in range(8):
        ids = dish_ref[c : c + 1, :]
        hot = peer == (spread(ids, PEERS) >> 6)
        n_lane = iota((PEERS, LANES), 1)
        left = jnp.concatenate(
            [jnp.where(hot, float(c), 0.0), jnp.where(hot, n_lane, 0).astype(F32)], axis=0
        )
        right = (spread(ids, LANES) & 63) == (low & 63)
        acc = acc + lax.dot_general(
            left.astype(BF16), right.astype(F32).astype(BF16), nt, preferred_element_type=F32
        )
    idx_ref[32:64, :] = (acc + 0.5).astype(I32)
    acc = jnp.zeros((2 * PEERS, LANES), F32)
    for c in range(16):
        ids = spread(group_ref[c : c + 1, :], PEERS)
        zone = div124(ids)
        n = LANES * c + iota((PEERS, LANES), 1)
        hot = (peer == zone) & (n < GROUPS)
        dy = div63(n + 32)
        dx = n + 32 - 63 * dy - 31
        table_row = dy >> 1
        table_lane = 64 * (dy & 1) + (dx & 63)
        left = jnp.concatenate(
            [jnp.where(hot, table_row, 0), jnp.where(hot, table_lane, 0)], axis=0
        ).astype(F32)
        rest = (ids - 124 * zone)[0:1, :]
        right = spread(rest, LANES) == low
        acc = acc + lax.dot_general(
            left.astype(BF16), right.astype(F32).astype(BF16), nt, preferred_element_type=F32
        )
    idx_ref[64:96, :] = (acc + 0.5).astype(I32)
    for g in range(SLOT_GROUPS):
        pairs = blocks_ref[8 * g : 8 * g + 8, :] if g < 4 else blocks_ref[32:33, :]
        gap = jnp.broadcast_to(pairs[:, 1:2] - pairs[:, 0:1], (8, LANES))
        for j in range(8):
            cols = slice(LANES * j, LANES * j + LANES)
            first_col = 4 * j + (lane >> 5)
            second_col = lane & 31
            ok = (gap > 0) | (second_col > first_col)
            if g < 4:
                w = weights_ref[8 * g : 8 * g + 8, cols]
            else:
                w = spread(weights_ref[32:33, cols])
                ok = ok & (sub == 0)
            wts_ref[8 * g : 8 * g + 8, cols] = jnp.where(ok, w.astype(F32), 0.0) * (1.0 / 32.0)
    lane16 = iota((PEERS, LANES), 1)
    one = spread(turned_ref[0:1, :], PEERS)
    two = spread(turned_ref[1:2, :], PEERS)
    ends = jnp.where(lane16 < 40, one, pltpu.roll(two, 40, axis=1))
    hot_ref[0:16, :] = jnp.where((ends >> 2) == peer, 1.0, 0.0).astype(BF16)
    hot_ref[16:32, :] = jnp.where(((two - one) >> 1) == peer, 1.0, 0.0).astype(BF16)
    k = iota((LANES, LANES), 0)
    l = iota((LANES, LANES), 1)
    e2_ref[...] = jnp.where(((k & 31) == (l & 31)) & (k < 96), 1.0, 0.0).astype(BF16)
    for j in range(8):
        cols = slice(LANES * j, LANES * j + LANES)
        c1 = 4 * j + (l >> 5)
        e1_ref[:, cols] = jnp.where(((k & 31) == c1) & (k < 96), 1.0, 0.0).astype(BF16)
        same = (k & 63) == (((l & 31) - c1) & 63)
        ey_ref[0:128, cols] = jnp.where(same, 1.0, 0.0).astype(BF16)
        ey_ref[128:256, cols] = jnp.where(same & (k < 64), 1.0, 0.0).astype(BF16)
        row1 = 4 * j + (k >> 5)
        s1_ref[cols, :] = jnp.where((l & 31) == row1, 1.0, 0.0).astype(BF16)
        sd_ref[cols, :] = jnp.where((l & 63) == (((k & 31) - row1) & 63), 1.0, 0.0).astype(BF16)


def main_kernel(
    recv_ref, dish_ref, blocks_ref, idx_ref, wts_ref, hot_ref, e1_ref, e2_ref, ey_ref, s1_ref, sd_ref,
    tan_ref, before_ref, after_ref,
    out_ref, prior_ref,
    gtab, ytab, la, lb, ly, ga, gb, yy, xf, xd, ff, gg, gout, yout,
):
    lane = iota((8, LANES), 1)
    quad = lane >> 5
    half = lane >> 6
    for p in range(2):
        t0 = tan_ref[p, 0:1, :]
        t1 = tan_ref[p, 1:2, :]
        prior_ref[p, 0:1, :] = PRIOR_WEIGHT * (2.0 * t0 - before_ref[p] - t1)
        prior_ref[p, 1:2, :] = PRIOR_WEIGHT * (2.0 * t1 - t0 - after_ref[p])
    dish = dish_ref[...]
    zone = dish >> 6
    at = dish & 63
    for b in range(4):
        res = [jnp.zeros((8, LANES), F32), jnp.zeros((8, LANES), F32)]
        for z in range(PEERS):
            row = spread(recv_ref[z, :, LANES * b : LANES * b + LANES])
            hit = zone == z
            for c in range(CHANS):
                res[c] = jnp.where(hit, by_lane(row, at + 64 * c), res[c])
        for c in range(CHANS):
            gtab[2 * b + c] = res[c]
    for b in range(8):
        res = [jnp.zeros((8, LANES), F32), jnp.zeros((8, LANES), F32)]
        for z in range(PEERS):
            row = spread(recv_ref[z, :, 512 + LANES * b : 512 + LANES * b + LANES])
            for h in range(2):
                hit = idx_ref[8 * h : 8 * h + 8, :] == z
                res[h] = jnp.where(hit, by_lane(row, idx_ref[16 + 8 * h : 24 + 8 * h, :]), res[h])
        ytab[b, 0:8, :] = res[0]
        ytab[b, 8:16, :] = res[1]
    ends = []
    for g in range(SLOT_GROUPS):
        pairs = blocks_ref[8 * g : 8 * g + 8, :] if g < 4 else blocks_ref[32:33, :]
        r1 = jnp.broadcast_to(pairs[:, 0:1], (8, LANES))
        r2 = jnp.broadcast_to(pairs[:, 1:2], (8, LANES))
        dy = r2 - r1
        ends.append((r1, r2, dy))
        for c in range(CHANS):
            for b in range(4):
                rows = slice(8 * ((2 * g + c) * 4 + b), 8 * ((2 * g + c) * 4 + b) + 8)
                table = gtab[2 * b + c]
                for r, dest in ((r1, la), (r2, lb)):
                    x = jnp.where((r & 3) == quad, by_sublane(table, r >> 2), 0.0)
                    x = x + pltpu.roll(x, 64, axis=1)
                    x = x + pltpu.roll(x, 32, axis=1)
                    hi, mid, lo = split3(x)
                    dest[rows, :] = jnp.where(quad == 0, hi, jnp.where(quad == 1, mid, lo))
                low = by_sublane(ytab[2 * b + c, 0:8, :], (dy >> 1) & 7)
                high = by_sublane(ytab[2 * b + c, 8:16, :], (dy >> 1) & 7)
                x = jnp.where((dy & 1) == half, jnp.where(dy < 16, low, high), 0.0)
                x = x + pltpu.roll(x, 64, axis=1)
                hi, mid, lo = split3(x)
                ly[rows, 0:128] = jnp.where(half == 0, hi, mid)
                ly[rows, 128:256] = lo
    ga[...] = jnp.dot(la[...].astype(BF16), e1_ref[...], preferred_element_type=F32)
    gb[...] = jnp.dot(lb[...].astype(BF16), e2_ref[...], preferred_element_type=F32)
    yy[...] = jnp.dot(ly[...].astype(BF16), ey_ref[...], preferred_element_type=F32)
    for g in range(SLOT_GROUPS):
        r1, r2, dy = ends[g]
        for c in range(CHANS):
            at_rows = [slice(8 * ((2 * g + c) * 4 + b), 8 * ((2 * g + c) * 4 + b) + 8) for b in range(4)]
            gbr, gbi, dbr, dbi = [gb[r, :] for r in at_rows]
            both = slice(16 * (2 * g + c), 16 * (2 * g + c) + 16)
            s_re = s_im = None
            for j in range(8):
                cols = slice(LANES * j, LANES * j + LANES)
                ga_r, ga_i, da_r, da_i = [ga[r, cols] for r in at_rows]
                y_r, y_i, t_r, t_i = [yy[r, cols] for r in at_rows]
                w = wts_ref[8 * g : 8 * g + 8, cols]
                p_r = ga_r * gbr + ga_i * gbi
                p_i = ga_i * gbr - ga_r * gbi
                q_r = (da_r * gbr + da_i * gbi) + (ga_r * dbr + ga_i * dbi)
                q_i = (da_i * gbr - da_r * gbi) + (ga_i * dbr - ga_r * dbi)
                u_r = w * ((q_r * y_r - q_i * y_i) + (p_r * t_r - p_i * t_i))
                u_i = w * ((q_r * y_i + q_i * y_r) + (p_r * t_i + p_i * t_r))
                v_r = u_r * y_r + u_i * y_i
                v_i = u_i * y_r - u_r * y_i
                f = jnp.concatenate([v_r * gbr - v_i * gbi, v_r * gbi + v_i * gbr], axis=0)
                a_r = v_r * ga_r + v_i * ga_i
                a_i = v_r * ga_i - v_i * ga_r
                d = jnp.concatenate([u_r * p_r + u_i * p_i, u_i * p_r - u_r * p_i], axis=0)
                for x, dest in ((f, xf), (d, xd)):
                    for k in range(PARTS):
                        part = x.astype(BF16)
                        dest[k, both, cols] = part
                        if k + 1 < PARTS:
                            x = x - part.astype(F32)
                s_re = a_r if j == 0 else s_re + a_r
                s_im = a_i if j == 0 else s_im + a_i
            for p, one in enumerate((s_re, s_im)):
                one = one + pltpu.roll(one, 64, axis=1)
                one = one + pltpu.roll(one, 32, axis=1)
                dest = slice(LANES * (2 * p + c), LANES * (2 * p + c + 1))
                ff[40 + 8 * g : 48 + 8 * g, dest] = jnp.where((r2 & 3) == quad, one, 0.0)
    first = jnp.dot(xf[0], s1_ref[...], preferred_element_type=F32)
    diag = jnp.dot(xd[0], sd_ref[...], preferred_element_type=F32)
    for k in range(1, PARTS):
        first = first + jnp.dot(xf[k], s1_ref[...], preferred_element_type=F32)
        diag = diag + jnp.dot(xd[k], sd_ref[...], preferred_element_type=F32)
    for g in range(SLOT_GROUPS):
        r1, r2, dy = ends[g]
        for c in range(CHANS):
            for p in range(2):
                rows = slice(16 * (2 * g + c) + 8 * p, 16 * (2 * g + c) + 8 * p + 8)
                dest = slice(LANES * (2 * p + c), LANES * (2 * p + c + 1))
                ff[8 * g : 8 * g + 8, dest] = jnp.where((r1 & 3) == quad, first[rows], 0.0)
                gg[8 * g : 8 * g + 8, dest] = jnp.where((dy & 1) == half, diag[rows], 0.0)
    gsum = ysum = None
    for fx, gx in zip(split3(ff[...]), split3(gg[...])):
        fk = jnp.dot(hot_ref[0:16, 0:80], fx.astype(BF16), preferred_element_type=F32)
        gk = jnp.dot(hot_ref[16:32, 0:40], gx.astype(BF16), preferred_element_type=F32)
        gsum = fk if gsum is None else gsum + fk
        ysum = gk if ysum is None else ysum + gk
    gout[...] = gsum[0:8]
    yout[...] = ysum
    for h in range(2):
        rows = slice(8 * h, 8 * h + 8)
        at_row = idx_ref[32 + 8 * h : 40 + 8 * h, :]
        at_lane = idx_ref[48 + 8 * h : 56 + 8 * h, :]
        for p in range(2):
            res = jnp.zeros((8, LANES), F32)
            for c in range(CHANS):
                mine = half == c
                for k in range(8):
                    row = spread(gout[k : k + 1, LANES * (2 * p + c) : LANES * (2 * p + c + 1)])
                    res = jnp.where(mine & (at_row == k), by_lane(row, at_lane), res)
            out_ref[rows, 0, 512 + LANES * p : 512 + LANES * (p + 1)] = res
        at_row = idx_ref[64 + 8 * h : 72 + 8 * h, :]
        at_lane = idx_ref[80 + 8 * h : 88 + 8 * h, :]
        for q in range(4):
            res = jnp.zeros((8, LANES), F32)
            for k in range(16):
                row = spread(yout[k : k + 1, LANES * q : LANES * (q + 1)])
                res = jnp.where(at_row == k, by_lane(row, at_lane), res)
            out_ref[rows, 0, LANES * q : LANES * (q + 1)] = res


def final_kernel(recv_ref, prior_ref, gain_ref, group_ref):
    for p in range(2):
        at = 512 + LANES * p
        total = recv_ref[0, :, at : at + LANES]
        for z in range(1, PEERS):
            total = total + recv_ref[z, :, at : at + LANES]
        for c in range(CHANS):
            gain_ref[p, c : c + 1, :] = total[:, 64 * c : 64 * c + 64] + prior_ref[p, c : c + 1, :]
            at_q = LANES * (2 * p + c)
            sums = recv_ref[0, :, at_q : at_q + LANES]
            for z in range(1, PEERS):
                sums = sums + recv_ref[z, :, at_q : at_q + LANES]
            group_ref[p, c : c + 1, :] = sums[:, 0:GROUP_PART]


def vmem(count):
    return [pl.BlockSpec(memory_space=pltpu.VMEM)] * count


def local(gains, gain_tan, group_vis, group_tan, dish_of, group_of, block_list, weights):
    shape = jax.ShapeDtypeStruct
    sent = pl.pallas_call(
        pack_kernel,
        in_specs=vmem(4),
        out_specs=vmem(1)[0],
        out_shape=shape((PEERS, 1, GATHER_WIDTH), F32),
        name="pack",
    )(gains, gain_tan, group_vis, group_tan)
    gathered = lax.all_to_all(sent, "bl", 0, 0, tiled=True)
    peers = lax.axis_size("tf")
    up = [(i, i + 1) for i in range(peers - 1)]
    down = [(j, i) for i, j in up]
    before = lax.ppermute(gain_tan[:, 1:2], "tf", up)
    after = lax.ppermute(gain_tan[:, 0:1], "tf", down)
    dish_table = dish_of.reshape(8, LANES)
    group_table = jnp.pad(group_of, (0, 16 * LANES - GROUPS)).reshape(16, LANES)
    turned = jnp.pad(block_list.T, ((0, 0), (0, LANES - SLOTS)))
    tables = pl.pallas_call(
        prep_kernel,
        in_specs=vmem(5),
        out_specs=vmem(8),
        out_shape=(
            shape((96, LANES), I32),
            shape((8 * SLOT_GROUPS, 1024), F32),
            shape((32, LANES), BF16),
            shape((LANES, 1024), BF16),
            shape((LANES, LANES), BF16),
            shape((2 * LANES, 1024), BF16),
            shape((1024, LANES), BF16),
            shape((1024, LANES), BF16),
        ),
        name="prep",
    )(dish_table, group_table, block_list, turned, weights)
    partial, prior = pl.pallas_call(
        main_kernel,
        in_specs=vmem(14),
        out_specs=vmem(2),
        out_shape=(shape((PEERS, 1, SCATTER_WIDTH), F32), shape((2, CHANS, DISH_PART), F32)),
        scratch_shapes=[
            pltpu.VMEM((8, 8, LANES), F32),
            pltpu.VMEM((8, 16, LANES), F32),
            pltpu.VMEM((ROWS_ALL, LANES), F32),
            pltpu.VMEM((ROWS_ALL, LANES), F32),
            pltpu.VMEM((ROWS_ALL, 2 * LANES), F32),
            pltpu.VMEM((ROWS_ALL, 1024), F32),
            pltpu.VMEM((ROWS_ALL, LANES), F32),
            pltpu.VMEM((ROWS_ALL, 1024), F32),
            pltpu.VMEM((PARTS, ROWS_ALL // 2, 1024), BF16),
            pltpu.VMEM((PARTS, ROWS_ALL // 2, 1024), BF16),
            pltpu.VMEM((80, 4 * LANES), F32),
            pltpu.VMEM((40, 4 * LANES), F32),
            pltpu.VMEM((8, 4 * LANES), F32),
            pltpu.VMEM((16, 4 * LANES), F32),
        ],
        name="main",
    )(gathered, dish_table, block_list, *tables, gain_tan, before, after)
    parts = lax.all_to_all(partial, "bl", 0, 0, tiled=True)
    return pl.pallas_call(
        final_kernel,
        in_specs=vmem(2),
        out_specs=vmem(2),
        out_shape=(shape((2, CHANS, DISH_PART), F32), shape((2, CHANS, GROUP_PART), F32)),
        name="finish",
    )(parts, prior)


def solution(mesh):
    placed = (
        P(None, "tf", "bl"),
        P(None, "tf", "bl"),
        P(None, "tf", "bl"),
        P(None, "tf", "bl"),
        P(),
        P(),
        P("bl", None),
        P("bl", None),
    )
    return jax.shard_map(
        local,
        mesh=mesh,
        in_specs=placed,
        out_specs=(P(None, "tf", "bl"), P(None, "tf", "bl")),
        check_vma=False,
    )
```

time: 68.6 us -> 61.7 us (0.90)
  the two profiles are of different devices: /device:TPU:24 before, /device:TPU:25 now
where the time goes in v2:
time: 61.7 us; the launch traced here: 60.6 us
  blocking collectives  23.1 us (37%)
  starting transfers between devices  22.7 us (37%)
  Pallas kernels  11.6 us (19%)
  local copies, waits for them, and re-layouts  2.52 us (4%)
  between operations  0.73 us (1%)
    all_to_all x1, blocking collectives, local(): parts = lax.all_to_all(partial, 'bl', 0, 0, tiled=True)  23.1 us
    all_to_all x1, starting transfers between devices, local(): gathered = lax.all_to_all(sent, 'bl', 0, 0, tiled=True)  15 us
    pallas_call x1, Pallas kernels, local(): pl.pallas_call(main_kernel, in_specs=vmem(14), out_specs=vmem(2), out_sha...  5.73 us
    ppermute x1, starting transfers between devices, local(): before = lax.ppermute(gain_tan[:, 1:2], 'tf', up)  4.81 us
    ppermute x1, starting transfers between devices, local(): after = lax.ppermute(gain_tan[:, 0:1], 'tf', down)  2.86 us
    pallas_call x1, Pallas kernels, local(): pl.pallas_call(prep_kernel, in_specs=vmem(5), out_specs=vmem(8), out_shap...  2.86 us
    pallas_call x1, Pallas kernels, local(): pl.pallas_call(final_kernel, in_specs=vmem(2), out_specs=vmem(2), out_sha...  1.52 us
    pallas_call x1, Pallas kernels, local(): pl.pallas_call(pack_kernel, in_specs=vmem(4), out_specs=vmem(1)[0], out_s...  1.47 us
  transfers between devices with their start and end apart: 3, of which 0 were waited for; matrix products, arithmetic and copies ran while one was open for 3% of the time, Pallas kernels for 5%

profile of v2, /device:TPU:25, one launch (start us, length us, event | category | flops | bytes accessed | tf_op | source)
XLA Modules:
  0.0 60.6 jit_solution(6813587304986272628)
XLA Ops:
  0.6 1.5 %pack.1 = f32[16,1,1536]{2,1,0:T(1,128)} custom-call(f32[2,2,64]{2,1,0:T(2,128)} %gain_ref.1, f32[2,2,64]{2,1,0:T(2,128)} %tan_ref.3, f32[2,2,124]{2,1,0:T(2,128)} %vis_ref.1, f32[2,2,124]{2,1,0:T(2,128)} %gtan_ref.1), custom_call_target="tpu_custom_call" | custom-call | tf_op jit(solution)/shard_map/pack/pallas_call | solution.py:334
  2.1 0.0 copy-start.1
  2.1 0.0 copy-start.2
  2.1 15.0 %all-to-all-start = ((f32[16,1,1536]{2,1,0:T(1,128)}), f32[16,1,1536]{2,1,0:T(1,128)S(1)}, u32[]{:S(2)}, u32[]{:S(2)}) async-start(f32[16,1,1536]{2,1,0:T(1,128)} %pack.1), calls=%async_computation | async-start | bytes 196608 | tf_op jit(solution)/shard_map/all_to_all | solution.py:341
  17.2 0.0 copy-done.1
  17.2 2.9 %collective-permute-start.1 = (f32[2,1,64]{2,1,0:T(1,128)S(1)}, f32[2,1,64]{2,1,0:T(1,128)S(1)}, u32[]{:S(2)}, u32[]{:S(2)}) collective-permute-start(f32[2,1,64]{2,1,0:T(1,128)S(1)} %get-tuple-element.22), channel_id=1, source_target_pairs={{16,0},{32,16},{48,32},{64,48},{80,64},{96,80},{112,96},{128,112},... | collective-permute-start | bytes 1544 | tf_op jit(solution)/shard_map/ppermute | solution.py:346
  20.0 0.0 copy-start.3
  20.1 4.8 %collective-permute-start = (f32[2,1,64]{2,1,0:T(1,128)S(1)}, f32[2,1,64]{2,1,0:T(1,128)S(1)}, u32[]{:S(2)}, u32[]{:S(2)}) collective-permute-start(f32[2,1,64]{2,1,0:T(1,128)S(1)} %get-tuple-element.23), channel_id=1, source_target_pairs={{0,16},{16,32},{32,48},{48,64},{64,80},{80,96},{96,112},{112,128},... | collective-permute-start | bytes 1544 | tf_op jit(solution)/shard_map/ppermute | solution.py:345
  24.9 0.0 copy-done.2
  24.9 0.6 pad_bitcast_fusion.group_ref
  25.5 0.0 copy-done.3
  25.5 0.7 %copy.11.blocks_ref = s32[33,2]{1,0:T(8,128)} copy(s32[33,2]{0,1:T(2,128)S(1)} %copy-done.3) | data formatting | bytes 528 | tf_op args[6]
  26.2 0.6 pad.9.turned_ref
  26.7 2.9 %prep.1 = (s32[96,128]{1,0:T(8,128)}, f32[40,1024]{1,0:T(8,128)}, bf16[32,128]{1,0:T(8,128)(2,1)}, bf16[128,1024]{1,0:T(8,128)(2,1)}, bf16[128,128]{1,0:T(8,128)...) custom-call(s32[8,128]{1,0:T(8,128)} %bitcast.4, ...), custom_call_target="tpu_custom_call" | custom-call | tf_op jit(solution)/shard_map/prep/pallas_call | solution.py:350
  29.6 0.0 collective-permute-done.1.after_ref
  29.6 0.0 copy-start.4
  29.6 0.0 collective-permute-done.before_ref
  29.6 0.0 copy-start.5
  29.6 0.0 all-to-all-done.recv_ref
  29.7 0.0 copy-start
  29.7 0.5 copy-done.4
  30.2 0.0 copy-done.5
  30.2 0.1 copy-done
  30.3 5.7 %main.1 = (f32[16,1,768]{2,1,0:T(1,128)}, f32[2,2,64]{2,1,0:T(2,128)}) custom-call(f32[16,1,1536]{2,1,0:T(1,128)} %copy-done, s32[8,128]{1,0:T(8,128)} %bitcast.5, s32[33,2]{1,0:T(8,128)} %copy.11.blocks_ref, s32[96,128]{1,0:T(8,128)} %get-tuple-element.12.idx_ref, f32[40,1024]{1,0:T(8,128)} %get-tuple-element.13.wts_ref, ...), custom_call_target="tpu_custom_call" | custom-call | tf_op jit(solution)/shard_map/main/pallas_call | solution.py:366
  36.0 23.1 %all_to_all.10.recv_ref = f32[16,1,768]{2,1,0:T(1,128)} all-to-all(f32[16,1,768]{2,1,0:T(1,128)} %get-tuple-element.20), channel_id=1, replica_groups=mesh['tf'=32,'bl'=16] {'bl'}, dimensions={0} | all-to-all | bytes 98304 | tf_op jit(solution)/shard_map/all_to_all | solution.py:389
  59.1 1.5 %finish.1 = (f32[2,2,64]{2,1,0:T(2,128)}, f32[2,2,124]{2,1,0:T(2,128)}) custom-call(f32[16,1,768]{2,1,0:T(1,128)} %all_to_all.10.recv_ref, f32[2,2,64]{2,1,0:T(2,128)} %get-tuple-element.21.prior_ref), custom_call_target="tpu_custom_call" | custom-call | tf_op jit(solution)/shard_map/finish/pallas_call | solution.py:390
  (1 shorter events, 0.0 us)
Async XLA Ops:
  2.1 15.1 %copy-start.1 = (f32[2,2,64]{2,1,0:T(2,128)S(1)}, f32[2,2,64]{2,1,0:T(2,128)}, u32[]{:S(2)}) copy-start(f32[2,2,64]{2,1,0:T(2,128)} %tan_ref.3) | copy-start | bytes 3076
  2.1 22.8 %copy-start.2 = (s32[1984]{0:T(1024)S(1)}, s32[1984]{0:T(1024)}, u32[]{:S(2)}) copy-start(s32[1984]{0:T(1024)} %param.13) | copy-start | bytes 23812
  2.1 27.6 %all-to-all-start = ((f32[16,1,1536]{2,1,0:T(1,128)}), f32[16,1,1536]{2,1,0:T(1,128)S(1)}, u32[]{:S(2)}, u32[]{:S(2)}) async-start(f32[16,1,1536]{2,1,0:T(1,128)} %pack.1), calls=%async_computation | async-start | bytes 196608 | tf_op jit(solution)/shard_map/all_to_all | solution.py:341
  17.2 12.4 %collective-permute-start.1 = (f32[2,1,64]{2,1,0:T(1,128)S(1)}, f32[2,1,64]{2,1,0:T(1,128)S(1)}, u32[]{:S(2)}, u32[]{:S(2)}) collective-permute-start(f32[2,1,64]{2,1,0:T(1,128)S(1)} %get-tuple-element.22), channel_id=1, source_target_pairs={{16,0},{32,16},{48,32},{64,48},{80,64},{96,80},{112,96},{128,112},... | collective-permute-start | bytes 1544 | tf_op jit(solution)/shard_map/ppermute | solution.py:346
  20.0 5.4 %copy-start.3 = (s32[33,2]{0,1:T(2,128)S(1)}, s32[33,2]{0,1:T(2,128)}, u32[]{:S(2)}) copy-start(s32[33,2]{0,1:T(2,128)} %param.14) | copy-start | bytes 796
  20.1 9.6 %collective-permute-start = (f32[2,1,64]{2,1,0:T(1,128)S(1)}, f32[2,1,64]{2,1,0:T(1,128)S(1)}, u32[]{:S(2)}, u32[]{:S(2)}) collective-permute-start(f32[2,1,64]{2,1,0:T(1,128)S(1)} %get-tuple-element.23), channel_id=1, source_target_pairs={{0,16},{16,32},{32,48},{48,64},{64,80},{80,96},{96,112},{112,128},... | collective-permute-start | bytes 1544 | tf_op jit(solution)/shard_map/ppermute | solution.py:345
  29.6 0.6 copy-start.4
  29.6 0.6 copy-start.5
  29.7 0.6 %copy-start = (f32[16,1,1536]{2,1,0:T(1,128)}, f32[16,1,1536]{2,1,0:T(1,128)S(1)}, u32[]{:S(2)}) copy-start(f32[16,1,1536]{2,1,0:T(1,128)S(1)} %all-to-all-done.recv_ref) | copy-start | bytes 294916

commit v3 on v2

--- a/solution.py
+++ b/solution.py
@@ -20,7 +20,7 @@
 SLOT_GROUPS = 5
 GATHER_WIDTH = 1536
 SCATTER_WIDTH = 768
-PARTS = 3
+PARTS = 2
 
 F32 = jnp.float32
 I32 = jnp.int32
@@ -77,7 +77,7 @@
 
 def prep_kernel(
     dish_ref, group_ref, blocks_ref, turned_ref, weights_ref,
-    idx_ref, wts_ref, hot_ref, e1_ref, e2_ref, ey_ref, s1_ref, sd_ref,
+    idx_ref, ends_ref, wts_ref, hot_ref, e1_ref, e2_ref, ey_ref, s1_ref, sd_ref,
 ):
     lane = iota((8, LANES), 1)
     sub = iota((8, LANES), 0)
@@ -101,19 +101,21 @@
     peer = iota((PEERS, LANES), 0)
     low = iota((LANES, LANES), 0)
     nt = (((1,), (1,)), ((), ()))
-    acc = jnp.zeros((2 * PEERS, LANES), F32)
+    acc = jnp.zeros((PEERS, LANES), F32)
     for c in range(8):
-        ids = dish_ref[c : c + 1, :]
-        hot = peer == (spread(ids, PEERS) >> 6)
-        n_lane = iota((PEERS, LANES), 1)
+        ids = spread(dish_ref[c : c + 1, :])
+        hot = sub == ((ids >> 6) & 7)
         left = jnp.concatenate(
-            [jnp.where(hot, float(c), 0.0), jnp.where(hot, n_lane, 0).astype(F32)], axis=0
+            [jnp.where(hot, float(c), 0.0), jnp.where(hot, lane, 0).astype(F32)], axis=0
         )
-        right = (spread(ids, LANES) & 63) == (low & 63)
+        right = spread((ids & 63)[0:1] + 64 * (ids >> 9)[0:1], LANES) == low
         acc = acc + lax.dot_general(
             left.astype(BF16), right.astype(F32).astype(BF16), nt, preferred_element_type=F32
         )
-    idx_ref[32:64, :] = (acc + 0.5).astype(I32)
+    idx_ref[32:48, :] = (acc + 0.5).astype(I32)
+    dish = dish_ref[...]
+    idx_ref[80:88, :] = (dish >> 6) & 7
+    idx_ref[88:96, :] = (dish & 63) + 64 * (dish >> 9)
     acc = jnp.zeros((2 * PEERS, LANES), F32)
     for c in range(16):
         ids = spread(group_ref[c : c + 1, :], PEERS)
@@ -132,10 +134,15 @@
         acc = acc + lax.dot_general(
             left.astype(BF16), right.astype(F32).astype(BF16), nt, preferred_element_type=F32
         )
-    idx_ref[64:96, :] = (acc + 0.5).astype(I32)
+    idx_ref[48:80, :] = (acc + 0.5).astype(I32)
     for g in range(SLOT_GROUPS):
         pairs = blocks_ref[8 * g : 8 * g + 8, :] if g < 4 else blocks_ref[32:33, :]
-        gap = jnp.broadcast_to(pairs[:, 1:2] - pairs[:, 0:1], (8, LANES))
+        one = jnp.broadcast_to(pairs[:, 0:1], (8, LANES))
+        two = jnp.broadcast_to(pairs[:, 1:2], (8, LANES))
+        gap = two - one
+        ends_ref[8 * g : 8 * g + 8, :] = one
+        ends_ref[40 + 8 * g : 48 + 8 * g, :] = two
+        ends_ref[80 + 8 * g : 88 + 8 * g, :] = gap
         for j in range(8):
             cols = slice(LANES * j, LANES * j + LANES)
             first_col = 4 * j + (lane >> 5)
@@ -169,31 +176,26 @@
 
 
 def main_kernel(
-    recv_ref, dish_ref, blocks_ref, idx_ref, wts_ref, hot_ref, e1_ref, e2_ref, ey_ref, s1_ref, sd_ref,
-    tan_ref, before_ref, after_ref,
-    out_ref, prior_ref,
-    gtab, ytab, la, lb, ly, ga, gb, yy, xf, xd, ff, gg, gout, yout,
+    recv_ref, idx_ref, ends_ref, wts_ref, hot_ref, e1_ref, e2_ref, ey_ref, s1_ref, sd_ref,
+    out_ref,
+    gsrc, gtab, ytab, la, lb, ly, ga, gb, yy, xf, xd, ff, gg, gout, yout,
 ):
     lane = iota((8, LANES), 1)
     quad = lane >> 5
     half = lane >> 6
-    for p in range(2):
-        t0 = tan_ref[p, 0:1, :]
-        t1 = tan_ref[p, 1:2, :]
-        prior_ref[p, 0:1, :] = PRIOR_WEIGHT * (2.0 * t0 - before_ref[p] - t1)
-        prior_ref[p, 1:2, :] = PRIOR_WEIGHT * (2.0 * t1 - t0 - after_ref[p])
-    dish = dish_ref[...]
-    zone = dish >> 6
-    at = dish & 63
+    at_row = idx_ref[80:88, :]
+    at_lane = idx_ref[88:96, :]
+    left = half == 0
     for b in range(4):
-        res = [jnp.zeros((8, LANES), F32), jnp.zeros((8, LANES), F32)]
-        for z in range(PEERS):
-            row = spread(recv_ref[z, :, LANES * b : LANES * b + LANES])
-            hit = zone == z
-            for c in range(CHANS):
-                res[c] = jnp.where(hit, by_lane(row, at + 64 * c), res[c])
-        for c in range(CHANS):
-            gtab[2 * b + c] = res[c]
+        one = recv_ref[0:8, 0, LANES * b : LANES * b + LANES]
+        two = recv_ref[8:16, 0, LANES * b : LANES * b + LANES]
+        gsrc[2 * b] = jnp.where(left, one, pltpu.roll(two, 64, axis=1))
+        gsrc[2 * b + 1] = jnp.where(left, pltpu.roll(one, 64, axis=1), two)
+    for q in range(8):
+        res = by_lane(spread(gsrc[q, 0:1, :]), at_lane)
+        for k in range(1, 8):
+            res = jnp.where(at_row == k, by_lane(spread(gsrc[q, k : k + 1, :]), at_lane), res)
+        gtab[q] = res
     for b in range(8):
         res = [jnp.zeros((8, LANES), F32), jnp.zeros((8, LANES), F32)]
         for z in range(PEERS):
@@ -205,10 +207,9 @@
         ytab[b, 8:16, :] = res[1]
     ends = []
     for g in range(SLOT_GROUPS):
-        pairs = blocks_ref[8 * g : 8 * g + 8, :] if g < 4 else blocks_ref[32:33, :]
-        r1 = jnp.broadcast_to(pairs[:, 0:1], (8, LANES))
-        r2 = jnp.broadcast_to(pairs[:, 1:2], (8, LANES))
-        dy = r2 - r1
+        r1 = ends_ref[8 * g : 8 * g + 8, :]
+        r2 = ends_ref[40 + 8 * g : 48 + 8 * g, :]
+        dy = ends_ref[80 + 8 * g : 88 + 8 * g, :]
         ends.append((r1, r2, dy))
         for c in range(CHANS):
             for b in range(4):
@@ -288,41 +289,50 @@
         ysum = gk if ysum is None else ysum + gk
     gout[...] = gsum[0:8]
     yout[...] = ysum
+    at_row = idx_ref[32:40, :]
+    at_lane = idx_ref[40:48, :]
+    for p in range(2):
+        res = []
+        for c in range(CHANS):
+            cols = slice(LANES * (2 * p + c), LANES * (2 * p + c + 1))
+            one = by_lane(spread(gout[0:1, cols]), at_lane)
+            for k in range(1, 8):
+                one = jnp.where(at_row == k, by_lane(spread(gout[k : k + 1, cols]), at_lane), one)
+            res.append(one)
+        dest = slice(512 + LANES * p, 512 + LANES * (p + 1))
+        out_ref[0:8, 0, dest] = jnp.where(left, res[0], pltpu.roll(res[1], 64, axis=1))
+        out_ref[8:16, 0, dest] = jnp.where(left, pltpu.roll(res[0], 64, axis=1), res[1])
     for h in range(2):
-        rows = slice(8 * h, 8 * h + 8)
-        at_row = idx_ref[32 + 8 * h : 40 + 8 * h, :]
-        at_lane = idx_ref[48 + 8 * h : 56 + 8 * h, :]
-        for p in range(2):
-            res = jnp.zeros((8, LANES), F32)
-            for c in range(CHANS):
-                mine = half == c
-                for k in range(8):
-                    row = spread(gout[k : k + 1, LANES * (2 * p + c) : LANES * (2 * p + c + 1)])
-                    res = jnp.where(mine & (at_row == k), by_lane(row, at_lane), res)
-            out_ref[rows, 0, 512 + LANES * p : 512 + LANES * (p + 1)] = res
-        at_row = idx_ref[64 + 8 * h : 72 + 8 * h, :]
-        at_lane = idx_ref[80 + 8 * h : 88 + 8 * h, :]
+        at_row = idx_ref[48 + 8 * h : 56 + 8 * h, :]
+        at_lane = idx_ref[64 + 8 * h : 72 + 8 * h, :]
         for q in range(4):
-            res = jnp.zeros((8, LANES), F32)
-            for k in range(16):
-                row = spread(yout[k : k + 1, LANES * q : LANES * (q + 1)])
-                res = jnp.where(at_row == k, by_lane(row, at_lane), res)
-            out_ref[rows, 0, LANES * q : LANES * (q + 1)] = res
-
-
-def final_kernel(recv_ref, prior_ref, gain_ref, group_ref):
+            cols = slice(LANES * q, LANES * (q + 1))
+            res = by_lane(spread(yout[0:1, cols]), at_lane)
+            for k in range(1, 16):
+                res = jnp.where(at_row == k, by_lane(spread(yout[k : k + 1, cols]), at_lane), res)
+            out_ref[8 * h : 8 * h + 8, 0, cols] = res
+
+
+def final_kernel(recv_ref, tan_ref, before_ref, after_ref, gain_ref, group_ref):
     for p in range(2):
+        t0 = tan_ref[p, 0:1, :]
+        t1 = tan_ref[p, 1:2, :]
+        prior = [2.0 * t0 - before_ref[p] - t1, 2.0 * t1 - t0 - after_ref[p]]
         at = 512 + LANES * p
         total = recv_ref[0, :, at : at + LANES]
         for z in range(1, PEERS):
             total = total + recv_ref[z, :, at : at + LANES]
         for c in range(CHANS):
-            gain_ref[p, c : c + 1, :] = total[:, 64 * c : 64 * c + 64] + prior_ref[p, c : c + 1, :]
+            gain_ref[p, c : c + 1, :] = total[:, 64 * c : 64 * c + 64] + PRIOR_WEIGHT * prior[c]
             at_q = LANES * (2 * p + c)
             sums = recv_ref[0, :, at_q : at_q + LANES]
             for z in range(1, PEERS):
                 sums = sums + recv_ref[z, :, at_q : at_q + LANES]
             group_ref[p, c : c + 1, :] = sums[:, 0:GROUP_PART]
+
+
+def near(x):
+    return pltpu.with_memory_space_constraint(x, pltpu.VMEM)
 
 
 def vmem(count):
@@ -335,7 +345,7 @@
         pack_kernel,
         in_specs=vmem(4),
         out_specs=vmem(1)[0],
-        out_shape=shape((PEERS, 1, GATHER_WIDTH), F32),
+        out_shape=pltpu.VMEM((PEERS, 1, GATHER_WIDTH), F32),
         name="pack",
     )(gains, gain_tan, group_vis, group_tan)
     gathered = lax.all_to_all(sent, "bl", 0, 0, tiled=True)
@@ -350,25 +360,27 @@
     tables = pl.pallas_call(
         prep_kernel,
         in_specs=vmem(5),
-        out_specs=vmem(8),
+        out_specs=vmem(9),
         out_shape=(
-            shape((96, LANES), I32),
-            shape((8 * SLOT_GROUPS, 1024), F32),
-            shape((32, LANES), BF16),
-            shape((LANES, 1024), BF16),
-            shape((LANES, LANES), BF16),
-            shape((2 * LANES, 1024), BF16),
-            shape((1024, LANES), BF16),
-            shape((1024, LANES), BF16),
+            pltpu.VMEM((96, LANES), I32),
+            pltpu.VMEM((120, LANES), I32),
+            pltpu.VMEM((8 * SLOT_GROUPS, 1024), F32),
+            pltpu.VMEM((32, LANES), BF16),
+            pltpu.VMEM((LANES, 1024), BF16),
+            pltpu.VMEM((LANES, LANES), BF16),
+            pltpu.VMEM((2 * LANES, 1024), BF16),
+            pltpu.VMEM((1024, LANES), BF16),
+            pltpu.VMEM((1024, LANES), BF16),
         ),
         name="prep",
     )(dish_table, group_table, block_list, turned, weights)
-    partial, prior = pl.pallas_call(
+    partial = pl.pallas_call(
         main_kernel,
-        in_specs=vmem(14),
-        out_specs=vmem(2),
-        out_shape=(shape((PEERS, 1, SCATTER_WIDTH), F32), shape((2, CHANS, DISH_PART), F32)),
+        in_specs=vmem(10),
+        out_specs=vmem(1)[0],
+        out_shape=pltpu.VMEM((PEERS, 1, SCATTER_WIDTH), F32),
         scratch_shapes=[
+            pltpu.VMEM((8, 8, LANES), F32),
             pltpu.VMEM((8, 8, LANES), F32),
             pltpu.VMEM((8, 16, LANES), F32),
             pltpu.VMEM((ROWS_ALL, LANES), F32),
@@ -385,15 +397,15 @@
             pltpu.VMEM((16, 4 * LANES), F32),
         ],
         name="main",
-    )(gathered, dish_table, block_list, *tables, gain_tan, before, after)
+    )(near(gathered), *[near(a) for a in tables])
     parts = lax.all_to_all(partial, "bl", 0, 0, tiled=True)
     return pl.pallas_call(
         final_kernel,
-        in_specs=vmem(2),
+        in_specs=vmem(4),
         out_specs=vmem(2),
         out_shape=(shape((2, CHANS, DISH_PART), F32), shape((2, CHANS, GROUP_PART), F32)),
         name="finish",
-    )(parts, prior)
+    )(near(parts), near(gain_tan), near(before), near(after))
 
 
 def solution(mesh):

time: 61.7 us -> 52.1 us (0.84)
  the two profiles are of different devices: /device:TPU:25 before, /device:TPU:24 now
where the time goes in v3:
time: 52.1 us; the launch traced here: 51.8 us
  starting transfers between devices  24.5 us (47%)
  waiting for transfers between devices  17.1 us (33%)
  Pallas kernels  7.61 us (15%)
  local copies, waits for them, and re-layouts  1.87 us (4%)
  between operations  0.71 us (1%)
    all_to_all x1, starting transfers between devices, local(): gathered = lax.all_to_all(sent, 'bl', 0, 0, tiled=True)  15.3 us
    all_to_all x1, waiting for transfers between devices, local(): gathered = lax.all_to_all(sent, 'bl', 0, 0, tiled=True)  10 us
    all_to_all x1, waiting for transfers between devices, local(): parts = lax.all_to_all(partial, 'bl', 0, 0, tiled=True)  5.78 us
    pallas_call x1, Pallas kernels, local(): pl.pallas_call(main_kernel, in_specs=vmem(10), out_specs=vmem(1)[0], out_...  3.68 us
    ppermute x1, starting transfers between devices, local(): after = lax.ppermute(gain_tan[:, 0:1], 'tf', down)  3.64 us
    all_to_all x1, starting transfers between devices, local(): parts = lax.all_to_all(partial, 'bl', 0, 0, tiled=True)  3.63 us
    ppermute x1, starting transfers between devices, local(): before = lax.ppermute(gain_tan[:, 1:2], 'tf', up)  1.92 us
    pallas_call x1, Pallas kernels, local(): pl.pallas_call(prep_kernel, in_specs=vmem(5), out_specs=vmem(9), out_shap...  1.75 us
  transfers between devices with their start and end apart: 4, of which 3 were waited for; matrix products, arithmetic and copies ran while one was open for 4% of the time, Pallas kernels for 3%

profile of v3, /device:TPU:24, one launch (start us, length us, event | category | flops | bytes accessed | tf_op | source)
XLA Modules:
  0.0 51.8 jit_solution(17821674245427451761)
XLA Ops:
  0.6 1.5 %pack.1 = f32[16,1,1536]{2,1,0:T(1,128)} custom-call(f32[2,2,64]{2,1,0:T(2,128)} %gain_ref.1, f32[2,2,64]{2,1,0:T(2,128)} %tan_ref.3, f32[2,2,124]{2,1,0:T(2,128)} %vis_ref.1, f32[2,2,124]{2,1,0:T(2,128)} %gtan_ref.1), custom_call_target="tpu_custom_call" | custom-call | tf_op jit(solution)/shard_map/pack/pallas_call | solution.py:344
  2.1 0.0 copy-start.2
  2.1 15.3 %all-to-all-start = ((f32[16,1,1536]{2,1,0:T(1,128)}), f32[16,1,1536]{2,1,0:T(1,128)S(1)}, u32[]{:S(2)}, u32[]{:S(2)}) async-start(f32[16,1,1536]{2,1,0:T(1,128)} %pack.1), calls=%async_computation | async-start | bytes 196608 | tf_op jit(solution)/shard_map/all_to_all | solution.py:351
  17.4 0.0 copy-done.2
  17.4 0.0 copy-start.1
  17.4 0.7 %copy.10.blocks_ref = s32[33,2]{1,0:T(8,128)} copy(s32[33,2]{0,1:T(2,128)S(1)} %copy-done.2) | data formatting | bytes 528 | tf_op args[6]
  18.1 0.6 %pad.9.turned_ref = s32[2,128]{1,0:T(2,128)} pad(s32[2,33]{1,0:T(2,128)S(1)} %bitcast.5, s32[]{:T(128)} %constant.0.clone.1), padding=0_0x0_95 | pad | bytes 1292 | tf_op jit(solution)/shard_map/jit(_pad)/pad | solution.py:359
  18.7 0.0 copy-done.1
  18.7 0.6 %pad_bitcast_fusion.group_ref = s32[16,128]{1,0:T(8,128)} fusion(s32[1984]{0:T(1024)S(1)} %copy-done.1), kind=kLoop, calls=%fused_computation | loop fusion | bytes 16128 | tf_op jit(solution)/shard_map/reshape | solution.py:358
  19.3 1.8 %prep.1 = (s32[96,128]{1,0:T(8,128)S(1)}, s32[120,128]{1,0:T(8,128)S(1)}, f32[40,1024]{1,0:T(8,128)S(1)}, bf16[32,128]{1,0:T(8,128)(2,1)S(1)}, bf16[128,1024]{1,...) custom-call(s32[8,128]{1,0:T(8,128)} %bitcast.4, ...), custom_call_target="tpu_custom_call" | custom-call | tf_op jit(solution)/shard_map/prep/pallas_call | solution.py:360
  21.1 10.0 %all-to-all-done.recv_ref = f32[16,1,1536]{2,1,0:T(1,128)S(1)} async-done(((f32[16,1,1536]{2,1,0:T(1,128)}), f32[16,1,1536]{2,1,0:T(1,128)S(1)}, u32[]{:S(2)}, u32[]{:S(2)}) %all-to-all-start) | async-done | bytes 98336 | tf_op jit(solution)/shard_map/all_to_all | solution.py:351
  31.1 3.7 %main.1 = f32[16,1,768]{2,1,0:T(1,128)} custom-call(f32[16,1,1536]{2,1,0:T(1,128)S(1)} %all-to-all-done.recv_ref, s32[96,128]{1,0:T(8,128)S(1)} %get-tuple-element.11.idx_ref, s32[120,128]{1,0:T(8,128)S(1)} %get-tuple-element.12.ends_ref, f32[40,1024]{1,0:T(8,128)S(1)} %get-tuple-element.13.wts_ref, bf16[32,128]{1,0:T(8,128)(2,1)S(1)} %get-tuple-element.14.hot_ref, ...), custom_call_target="tpu_custom_call" | custom-call | tf_op jit(solution)/shard_map/main/pallas_call | solution.py:377
  34.8 0.0 copy-start
  34.8 3.6 %all-to-all-start.1 = ((f32[16,1,768]{2,1,0:T(1,128)}), f32[16,1,768]{2,1,0:T(1,128)S(1)}, u32[]{:S(2)}, u32[]{:S(2)}) async-start(f32[16,1,768]{2,1,0:T(1,128)} %main.1), calls=%async_computation.1 | async-start | bytes 98304 | tf_op jit(solution)/shard_map/all_to_all | solution.py:401
  38.4 0.0 copy-done
  38.4 1.9 %collective-permute-start = (f32[2,1,64]{2,1,0:T(1,128)S(1)}, f32[2,1,64]{2,1,0:T(1,128)S(1)}, u32[]{:S(2)}, u32[]{:S(2)}) collective-permute-start(f32[2,1,64]{2,1,0:T(1,128)S(1)} %get-tuple-element.21), channel_id=1, source_target_pairs={{0,16},{16,32},{32,48},{48,64},{64,80},{80,96},{96,112},{112,128},... | collective-permute-start | bytes 1544 | tf_op jit(solution)/shard_map/ppermute | solution.py:355
  40.3 3.6 %collective-permute-start.1 = (f32[2,1,64]{2,1,0:T(1,128)S(1)}, f32[2,1,64]{2,1,0:T(1,128)S(1)}, u32[]{:S(2)}, u32[]{:S(2)}) collective-permute-start(f32[2,1,64]{2,1,0:T(1,128)S(1)} %get-tuple-element.20), channel_id=1, source_target_pairs={{16,0},{32,16},{48,32},{64,48},{80,64},{96,80},{112,96},{128,112},... | collective-permute-start | bytes 1544 | tf_op jit(solution)/shard_map/ppermute | solution.py:356
  44.0 0.0 collective-permute-done.before_ref
  44.0 1.3 %collective-permute-done.1.after_ref = f32[2,1,64]{2,1,0:T(1,128)S(1)} collective-permute-done((f32[2,1,64]{2,1,0:T(1,128)S(1)}, f32[2,1,64]{2,1,0:T(1,128)S(1)}, u32[]{:S(2)}, u32[]{:S(2)}) %collective-permute-start.1) | collective-permute-done | bytes 544 | tf_op jit(solution)/shard_map/ppermute | solution.py:356
  45.3 5.8 %all-to-all-done.1.recv_ref = f32[16,1,768]{2,1,0:T(1,128)S(1)} async-done(((f32[16,1,768]{2,1,0:T(1,128)}), f32[16,1,768]{2,1,0:T(1,128)S(1)}, u32[]{:S(2)}, u32[]{:S(2)}) %all-to-all-start.1) | async-done | bytes 49184 | tf_op jit(solution)/shard_map/all_to_all | solution.py:401
  51.1 0.7 %finish.1 = (f32[2,2,64]{2,1,0:T(2,128)}, f32[2,2,124]{2,1,0:T(2,128)}) custom-call(f32[16,1,768]{2,1,0:T(1,128)S(1)} %all-to-all-done.1.recv_ref, f32[2,2,64]{2,1,0:T(2,128)S(1)} %copy-done, f32[2,1,64]{2,1,0:T(1,128)S(1)} %collective-permute-done.before_ref, f32[2,1,64]{2,1,0:T(1,128)S(1)} %collective-permute-done.1.after_ref), custom_call_target="tpu_custom_call" | custom-call | tf_op jit(solution)/shard_map/finish/pallas_call | solution.py:402
  (1 shorter events, 0.0 us)
Async XLA Ops:
  2.1 15.3 %copy-start.2 = (s32[33,2]{0,1:T(2,128)S(1)}, s32[33,2]{0,1:T(2,128)}, u32[]{:S(2)}) copy-start(s32[33,2]{0,1:T(2,128)} %param.14) | copy-start | bytes 796
  2.1 29.0 %all-to-all-start = ((f32[16,1,1536]{2,1,0:T(1,128)}), f32[16,1,1536]{2,1,0:T(1,128)S(1)}, u32[]{:S(2)}, u32[]{:S(2)}) async-start(f32[16,1,1536]{2,1,0:T(1,128)} %pack.1), calls=%async_computation | async-start | bytes 196608 | tf_op jit(solution)/shard_map/all_to_all | solution.py:351
  17.4 1.3 %copy-start.1 = (s32[1984]{0:T(1024)S(1)}, s32[1984]{0:T(1024)}, u32[]{:S(2)}) copy-start(s32[1984]{0:T(1024)} %param.13) | copy-start | bytes 23812
  34.8 3.6 %copy-start = (f32[2,2,64]{2,1,0:T(2,128)S(1)}, f32[2,2,64]{2,1,0:T(2,128)}, u32[]{:S(2)}) copy-start(f32[2,2,64]{2,1,0:T(2,128)} %tan_ref.3) | copy-start | bytes 3076
  34.8 16.3 %all-to-all-start.1 = ((f32[16,1,768]{2,1,0:T(1,128)}), f32[16,1,768]{2,1,0:T(1,128)S(1)}, u32[]{:S(2)}, u32[]{:S(2)}) async-start(f32[16,1,768]{2,1,0:T(1,128)} %main.1), calls=%async_computation.1 | async-start | bytes 98304 | tf_op jit(solution)/shard_map/all_to_all | solution.py:401
  38.4 5.6 %collective-permute-start = (f32[2,1,64]{2,1,0:T(1,128)S(1)}, f32[2,1,64]{2,1,0:T(1,128)S(1)}, u32[]{:S(2)}, u32[]{:S(2)}) collective-permute-start(f32[2,1,64]{2,1,0:T(1,128)S(1)} %get-tuple-element.21), channel_id=1, source_target_pairs={{0,16},{16,32},{32,48},{48,64},{64,80},{80,96},{96,112},{112,128},... | collective-permute-start | bytes 1544 | tf_op jit(solution)/shard_map/ppermute | solution.py:355
  40.3 4.9 %collective-permute-start.1 = (f32[2,1,64]{2,1,0:T(1,128)S(1)}, f32[2,1,64]{2,1,0:T(1,128)S(1)}, u32[]{:S(2)}, u32[]{:S(2)}) collective-permute-start(f32[2,1,64]{2,1,0:T(1,128)S(1)} %get-tuple-element.20), channel_id=1, source_target_pairs={{16,0},{32,16},{48,32},{64,48},{80,64},{96,80},{112,96},{128,112},... | collective-permute-start | bytes 1544 | tf_op jit(solution)/shard_map/ppermute | solution.py:356

commit v4 on v3

--- a/solution.py
+++ b/solution.py
@@ -21,6 +21,9 @@
 GATHER_WIDTH = 1536
 SCATTER_WIDTH = 768
 PARTS = 2
+LEAD = 12
+STEP = 1
+UNSTEP = 1
 
 F32 = jnp.float32
 I32 = jnp.int32
@@ -44,6 +47,10 @@
 
 def div63(n):
     return (n * 66577) >> 22
+
+
+def place(z):
+    return ((z - LEAD) * UNSTEP) & (PEERS - 1)
 
 
 def spread(row, rows=8):
@@ -96,7 +103,7 @@
             row = spread(group_ref[c : c + 1, :])
             found = jnp.where(chunk == c, by_lane(row, at), found)
         zg = div124(found)
-        idx_ref[8 * half : 8 * half + 8, :] = jnp.where(ok, zg, -1)
+        idx_ref[8 * half : 8 * half + 8, :] = jnp.where(ok, place(zg), -1)
         idx_ref[16 + 8 * half : 24 + 8 * half, :] = found - 124 * zg
     peer = iota((PEERS, LANES), 0)
     low = iota((LANES, LANES), 0)
@@ -104,24 +111,26 @@
     acc = jnp.zeros((PEERS, LANES), F32)
     for c in range(8):
         ids = spread(dish_ref[c : c + 1, :])
-        hot = sub == ((ids >> 6) & 7)
+        zone = place(ids >> 6)
+        hot = sub == (zone & 7)
         left = jnp.concatenate(
             [jnp.where(hot, float(c), 0.0), jnp.where(hot, lane, 0).astype(F32)], axis=0
         )
-        right = spread((ids & 63)[0:1] + 64 * (ids >> 9)[0:1], LANES) == low
+        right = spread((ids & 63)[0:1] + 64 * (zone >> 3)[0:1], LANES) == low
         acc = acc + lax.dot_general(
             left.astype(BF16), right.astype(F32).astype(BF16), nt, preferred_element_type=F32
         )
     idx_ref[32:48, :] = (acc + 0.5).astype(I32)
     dish = dish_ref[...]
-    idx_ref[80:88, :] = (dish >> 6) & 7
-    idx_ref[88:96, :] = (dish & 63) + 64 * (dish >> 9)
+    zone = place(dish >> 6)
+    idx_ref[80:88, :] = zone & 7
+    idx_ref[88:96, :] = (dish & 63) + 64 * (zone >> 3)
     acc = jnp.zeros((2 * PEERS, LANES), F32)
     for c in range(16):
         ids = spread(group_ref[c : c + 1, :], PEERS)
         zone = div124(ids)
         n = LANES * c + iota((PEERS, LANES), 1)
-        hot = (peer == zone) & (n < GROUPS)
+        hot = (peer == place(zone)) & (n < GROUPS)
         dy = div63(n + 32)
         dx = n + 32 - 63 * dy - 31
         table_row = dy >> 1
@@ -339,6 +348,11 @@
     return [pl.BlockSpec(memory_space=pltpu.VMEM)] * count
 
 
+def exchange(x):
+    order = [[(LEAD + i * STEP) % PEERS for i in range(PEERS)]]
+    return lax.all_to_all(x, "bl", 0, 0, axis_index_groups=order, tiled=True)
+
+
 def local(gains, gain_tan, group_vis, group_tan, dish_of, group_of, block_list, weights):
     shape = jax.ShapeDtypeStruct
     sent = pl.pallas_call(
@@ -348,7 +362,7 @@
         out_shape=pltpu.VMEM((PEERS, 1, GATHER_WIDTH), F32),
         name="pack",
     )(gains, gain_tan, group_vis, group_tan)
-    gathered = lax.all_to_all(sent, "bl", 0, 0, tiled=True)
+    gathered = exchange(sent)
     peers = lax.axis_size("tf")
     up = [(i, i + 1) for i in range(peers - 1)]
     down = [(j, i) for i, j in up]
@@ -398,7 +412,7 @@
         ],
         name="main",
     )(near(gathered), *[near(a) for a in tables])
-    parts = lax.all_to_all(partial, "bl", 0, 0, tiled=True)
+    parts = exchange(partial)
     return pl.pallas_call(
         final_kernel,
         in_specs=vmem(4),

time: 52.1 us -> 50.3 us (0.965)
  the two profiles are of different devices: /device:TPU:24 before, /device:TPU:25 now
where the time goes in v4:
time: 50.3 us; the launch traced here: 49.9 us
  starting transfers between devices  29.4 us (58%)
  waiting for transfers between devices  10.3 us (20%)
  Pallas kernels  7.61 us (15%)
  local copies, waits for them, and re-layouts  1.87 us (4%)
  between operations  0.69 us (1%)
    all_to_all x2, starting transfers between devices, exchange(): return lax.all_to_all(x, 'bl', 0, 0, axis_index_groups=order, tiled=True)  23.2 us
    all_to_all x2, waiting for transfers between devices, exchange(): return lax.all_to_all(x, 'bl', 0, 0, axis_index_groups=order, tiled=True)  5.26 us
    ppermute x1, waiting for transfers between devices, local(): after = lax.ppermute(gain_tan[:, 0:1], 'tf', down)  5.06 us
    ppermute x1, starting transfers between devices, local(): before = lax.ppermute(gain_tan[:, 1:2], 'tf', up)  4.33 us
    pallas_call x1, Pallas kernels, local(): pl.pallas_call(main_kernel, in_specs=vmem(10), out_specs=vmem(1)[0], out_...  3.67 us
    ppermute x1, starting transfers between devices, local(): after = lax.ppermute(gain_tan[:, 0:1], 'tf', down)  1.92 us
    pallas_call x1, Pallas kernels, local(): pl.pallas_call(prep_kernel, in_specs=vmem(5), out_specs=vmem(9), out_shap...  1.75 us
    pallas_call x1, Pallas kernels, local(): pl.pallas_call(pack_kernel, in_specs=vmem(4), out_specs=vmem(1)[0], out_s...  1.46 us
  transfers between devices with their start and end apart: 4, of which 2 were waited for; matrix products, arithmetic and copies ran while one was open for 4% of the time, Pallas kernels for 4%

profile of v4, /device:TPU:25, one launch (start us, length us, event | category | flops | bytes accessed | tf_op | source)
XLA Modules:
  0.0 49.9 jit_solution(10075842457976633887)
XLA Ops:
  0.6 1.5 %pack.1 = f32[16,1,1536]{2,1,0:T(1,128)} custom-call(f32[2,2,64]{2,1,0:T(2,128)} %gain_ref.1, f32[2,2,64]{2,1,0:T(2,128)} %tan_ref.3, f32[2,2,124]{2,1,0:T(2,128)} %vis_ref.1, f32[2,2,124]{2,1,0:T(2,128)} %gtan_ref.1), custom_call_target="tpu_custom_call" | custom-call | tf_op jit(solution)/shard_map/pack/pallas_call | solution.py:358
  2.1 0.0 copy-start.2
  2.1 15.2 %all-to-all-start = ((f32[16,1,1536]{2,1,0:T(1,128)}), f32[16,1,1536]{2,1,0:T(1,128)S(1)}, u32[]{:S(2)}, u32[]{:S(2)}) async-start(f32[16,1,1536]{2,1,0:T(1,128)} %pack.1), calls=%async_computation | async-start | bytes 196608 | tf_op jit(solution)/shard_map/all_to_all | solution.py:353
  17.3 0.0 copy-done.2
  17.3 0.0 copy-start.1
  17.3 0.7 %copy.10.blocks_ref = s32[33,2]{1,0:T(8,128)} copy(s32[33,2]{0,1:T(2,128)S(1)} %copy-done.2) | data formatting | bytes 528 | tf_op args[6]
  18.0 0.6 %pad.9.turned_ref = s32[2,128]{1,0:T(2,128)} pad(s32[2,33]{1,0:T(2,128)S(1)} %bitcast.5, s32[]{:T(128)} %constant.0.clone.1), padding=0_0x0_95 | pad | bytes 1292 | tf_op jit(solution)/shard_map/jit(_pad)/pad | solution.py:373
  18.6 0.0 copy-done.1
  18.6 0.6 %pad_bitcast_fusion.group_ref = s32[16,128]{1,0:T(8,128)} fusion(s32[1984]{0:T(1024)S(1)} %copy-done.1), kind=kLoop, calls=%fused_computation | loop fusion | bytes 16128 | tf_op jit(solution)/shard_map/reshape | solution.py:372
  19.2 1.7 %prep.1 = (s32[96,128]{1,0:T(8,128)S(1)}, s32[120,128]{1,0:T(8,128)S(1)}, f32[40,1024]{1,0:T(8,128)S(1)}, bf16[32,128]{1,0:T(8,128)(2,1)S(1)}, bf16[128,1024]{1,...) custom-call(s32[8,128]{1,0:T(8,128)} %bitcast.4, ...), custom_call_target="tpu_custom_call" | custom-call | tf_op jit(solution)/shard_map/prep/pallas_call | solution.py:374
  21.0 5.3 %all-to-all-done.recv_ref = f32[16,1,1536]{2,1,0:T(1,128)S(1)} async-done(((f32[16,1,1536]{2,1,0:T(1,128)}), f32[16,1,1536]{2,1,0:T(1,128)S(1)}, u32[]{:S(2)}, u32[]{:S(2)}) %all-to-all-start) | async-done | bytes 98336 | tf_op jit(solution)/shard_map/all_to_all | solution.py:353
  26.2 3.7 %main.1 = f32[16,1,768]{2,1,0:T(1,128)} custom-call(f32[16,1,1536]{2,1,0:T(1,128)S(1)} %all-to-all-done.recv_ref, s32[96,128]{1,0:T(8,128)S(1)} %get-tuple-element.11.idx_ref, s32[120,128]{1,0:T(8,128)S(1)} %get-tuple-element.12.ends_ref, f32[40,1024]{1,0:T(8,128)S(1)} %get-tuple-element.13.wts_ref, bf16[32,128]{1,0:T(8,128)(2,1)S(1)} %get-tuple-element.14.hot_ref, ...), custom_call_target="tpu_custom_call" | custom-call | tf_op jit(solution)/shard_map/main/pallas_call | solution.py:391
  29.9 0.0 copy-start
  29.9 7.9 %all-to-all-start.1 = ((f32[16,1,768]{2,1,0:T(1,128)}), f32[16,1,768]{2,1,0:T(1,128)S(1)}, u32[]{:S(2)}, u32[]{:S(2)}) async-start(f32[16,1,768]{2,1,0:T(1,128)} %main.1), calls=%async_computation.1 | async-start | bytes 98304 | tf_op jit(solution)/shard_map/all_to_all | solution.py:353
  37.8 0.0 copy-done
  37.9 4.3 %collective-permute-start = (f32[2,1,64]{2,1,0:T(1,128)S(1)}, f32[2,1,64]{2,1,0:T(1,128)S(1)}, u32[]{:S(2)}, u32[]{:S(2)}) collective-permute-start(f32[2,1,64]{2,1,0:T(1,128)S(1)} %get-tuple-element.21), channel_id=1, source_target_pairs={{0,16},{16,32},{32,48},{48,64},{64,80},{80,96},{96,112},{112,128},... | collective-permute-start | bytes 1544 | tf_op jit(solution)/shard_map/ppermute | solution.py:369
  42.2 1.9 %collective-permute-start.1 = (f32[2,1,64]{2,1,0:T(1,128)S(1)}, f32[2,1,64]{2,1,0:T(1,128)S(1)}, u32[]{:S(2)}, u32[]{:S(2)}) collective-permute-start(f32[2,1,64]{2,1,0:T(1,128)S(1)} %get-tuple-element.20), channel_id=1, source_target_pairs={{16,0},{32,16},{48,32},{64,48},{80,64},{96,80},{112,96},{128,112},... | collective-permute-start | bytes 1544 | tf_op jit(solution)/shard_map/ppermute | solution.py:370
  44.1 0.0 collective-permute-done.before_ref
  44.1 5.1 %collective-permute-done.1.after_ref = f32[2,1,64]{2,1,0:T(1,128)S(1)} collective-permute-done((f32[2,1,64]{2,1,0:T(1,128)S(1)}, f32[2,1,64]{2,1,0:T(1,128)S(1)}, u32[]{:S(2)}, u32[]{:S(2)}) %collective-permute-start.1) | collective-permute-done | bytes 544 | tf_op jit(solution)/shard_map/ppermute | solution.py:370
  49.2 0.0 all-to-all-done.1.recv_ref
  49.2 0.7 %finish.1 = (f32[2,2,64]{2,1,0:T(2,128)}, f32[2,2,124]{2,1,0:T(2,128)}) custom-call(f32[16,1,768]{2,1,0:T(1,128)S(1)} %all-to-all-done.1.recv_ref, f32[2,2,64]{2,1,0:T(2,128)S(1)} %copy-done, f32[2,1,64]{2,1,0:T(1,128)S(1)} %collective-permute-done.before_ref, f32[2,1,64]{2,1,0:T(1,128)S(1)} %collective-permute-done.1.after_ref), custom_call_target="tpu_custom_call" | custom-call | tf_op jit(solution)/shard_map/finish/pallas_call | solution.py:416
  (1 shorter events, 0.0 us)
Async XLA Ops:
  2.1 15.2 %copy-start.2 = (s32[33,2]{0,1:T(2,128)S(1)}, s32[33,2]{0,1:T(2,128)}, u32[]{:S(2)}) copy-start(s32[33,2]{0,1:T(2,128)} %param.14) | copy-start | bytes 796
  2.1 24.1 %all-to-all-start = ((f32[16,1,1536]{2,1,0:T(1,128)}), f32[16,1,1536]{2,1,0:T(1,128)S(1)}, u32[]{:S(2)}, u32[]{:S(2)}) async-start(f32[16,1,1536]{2,1,0:T(1,128)} %pack.1), calls=%async_computation | async-start | bytes 196608 | tf_op jit(solution)/shard_map/all_to_all | solution.py:353
  17.3 1.3 %copy-start.1 = (s32[1984]{0:T(1024)S(1)}, s32[1984]{0:T(1024)}, u32[]{:S(2)}) copy-start(s32[1984]{0:T(1024)} %param.13) | copy-start | bytes 23812
  29.9 8.0 %copy-start = (f32[2,2,64]{2,1,0:T(2,128)S(1)}, f32[2,2,64]{2,1,0:T(2,128)}, u32[]{:S(2)}) copy-start(f32[2,2,64]{2,1,0:T(2,128)} %tan_ref.3) | copy-start | bytes 3076
  29.9 19.3 %all-to-all-start.1 = ((f32[16,1,768]{2,1,0:T(1,128)}), f32[16,1,768]{2,1,0:T(1,128)S(1)}, u32[]{:S(2)}, u32[]{:S(2)}) async-start(f32[16,1,768]{2,1,0:T(1,128)} %main.1), calls=%async_computation.1 | async-start | bytes 98304 | tf_op jit(solution)/shard_map/all_to_all | solution.py:353
  37.9 6.3 %collective-permute-start = (f32[2,1,64]{2,1,0:T(1,128)S(1)}, f32[2,1,64]{2,1,0:T(1,128)S(1)}, u32[]{:S(2)}, u32[]{:S(2)}) collective-permute-start(f32[2,1,64]{2,1,0:T(1,128)S(1)} %get-tuple-element.21), channel_id=1, source_target_pairs={{0,16},{16,32},{32,48},{48,64},{64,80},{80,96},{96,112},{112,128},... | collective-permute-start | bytes 1544 | tf_op jit(solution)/shard_map/ppermute | solution.py:369
  42.2 7.0 %collective-permute-start.1 = (f32[2,1,64]{2,1,0:T(1,128)S(1)}, f32[2,1,64]{2,1,0:T(1,128)S(1)}, u32[]{:S(2)}, u32[]{:S(2)}) collective-permute-start(f32[2,1,64]{2,1,0:T(1,128)S(1)} %get-tuple-element.20), channel_id=1, source_target_pairs={{16,0},{32,16},{48,32},{64,48},{80,64},{96,80},{112,96},{128,112},... | collective-permute-start | bytes 1544 | tf_op jit(solution)/shard_map/ppermute | solution.py:370

commit v5 on v4

--- a/solution.py
+++ b/solution.py
@@ -154,15 +154,14 @@
         ends_ref[80 + 8 * g : 88 + 8 * g, :] = gap
         for j in range(8):
             cols = slice(LANES * j, LANES * j + LANES)
-            first_col = 4 * j + (lane >> 5)
-            second_col = lane & 31
-            ok = (gap > 0) | (second_col > first_col)
             if g < 4:
+                ok = (gap > 0) | ((lane & 31) > 4 * j + (lane >> 5))
                 w = weights_ref[8 * g : 8 * g + 8, cols]
+                wts_ref[8 * g : 8 * g + 8, cols] = jnp.where(ok, w.astype(F32), 0.0) * (1.0 / 32.0)
             else:
-                w = spread(weights_ref[32:33, cols])
-                ok = ok & (sub == 0)
-            wts_ref[8 * g : 8 * g + 8, cols] = jnp.where(ok, w.astype(F32), 0.0) * (1.0 / 32.0)
+                ok = (gap > 0) | ((lane & 31) > 4 * sub + (lane >> 5))
+                w = jnp.where(ok, spread(weights_ref[32:33, cols]).astype(F32), 0.0) * (1.0 / 32.0)
+                wts_ref[32 + j : 33 + j, 0:LANES] = w[j : j + 1]
     lane16 = iota((PEERS, LANES), 1)
     one = spread(turned_ref[0:1, :], PEERS)
     two = spread(turned_ref[1:2, :], PEERS)
@@ -171,7 +170,8 @@
     hot_ref[16:32, :] = jnp.where(((two - one) >> 1) == peer, 1.0, 0.0).astype(BF16)
     k = iota((LANES, LANES), 0)
     l = iota((LANES, LANES), 1)
-    e2_ref[...] = jnp.where(((k & 31) == (l & 31)) & (k < 96), 1.0, 0.0).astype(BF16)
+    e2_ref[0:128, :] = jnp.where(((k & 31) == (l & 31)) & (k < 96), 1.0, 0.0).astype(BF16)
+    e2_ref[128:256, :] = jnp.where(((k & 3) == (l >> 5)) & (k < 96), 1.0, 0.0).astype(BF16)
     for j in range(8):
         cols = slice(LANES * j, LANES * j + LANES)
         c1 = 4 * j + (l >> 5)
@@ -214,40 +214,56 @@
                 res[h] = jnp.where(hit, by_lane(row, idx_ref[16 + 8 * h : 24 + 8 * h, :]), res[h])
         ytab[b, 0:8, :] = res[0]
         ytab[b, 8:16, :] = res[1]
-    ends = []
+    def part_rows(g, c, k):
+        at = 128 * k + 32 * g + 16 * c if g < 4 else 256 + 32 * k + 16 * c
+        return slice(at, at + 16)
+
+    def sums(rows, width, x, table):
+        both = jnp.dot(x[rows, 0:width], table[0:width, :], preferred_element_type=F32)
+        return both[0 : both.shape[0] // 2] + both[both.shape[0] // 2 :]
+
+    sub = iota((8, LANES), 0)
     for g in range(SLOT_GROUPS):
+        lone = g == SLOT_GROUPS - 1
         r1 = ends_ref[8 * g : 8 * g + 8, :]
         r2 = ends_ref[40 + 8 * g : 48 + 8 * g, :]
         dy = ends_ref[80 + 8 * g : 88 + 8 * g, :]
-        ends.append((r1, r2, dy))
         for c in range(CHANS):
             for b in range(4):
-                rows = slice(8 * ((2 * g + c) * 4 + b), 8 * ((2 * g + c) * 4 + b) + 8)
+                at = 64 * g + 32 * c + 8 * b
+                rows = slice(at, at + 8)
                 table = gtab[2 * b + c]
                 for r, dest in ((r1, la), (r2, lb)):
                     x = jnp.where((r & 3) == quad, by_sublane(table, r >> 2), 0.0)
                     x = x + pltpu.roll(x, 64, axis=1)
                     x = x + pltpu.roll(x, 32, axis=1)
+                    if lone and dest is la:
+                        x = jnp.where(((lane >> 2) & 7) == sub, x, 0.0)
                     hi, mid, lo = split3(x)
                     dest[rows, :] = jnp.where(quad == 0, hi, jnp.where(quad == 1, mid, lo))
                 low = by_sublane(ytab[2 * b + c, 0:8, :], (dy >> 1) & 7)
                 high = by_sublane(ytab[2 * b + c, 8:16, :], (dy >> 1) & 7)
                 x = jnp.where((dy & 1) == half, jnp.where(dy < 16, low, high), 0.0)
                 x = x + pltpu.roll(x, 64, axis=1)
+                if lone:
+                    x = pltpu.roll(x, 0, axis=1, stride=4, stride_axis=0)
                 hi, mid, lo = split3(x)
                 ly[rows, 0:128] = jnp.where(half == 0, hi, mid)
                 ly[rows, 128:256] = lo
-    ga[...] = jnp.dot(la[...].astype(BF16), e1_ref[...], preferred_element_type=F32)
-    gb[...] = jnp.dot(lb[...].astype(BF16), e2_ref[...], preferred_element_type=F32)
-    yy[...] = jnp.dot(ly[...].astype(BF16), ey_ref[...], preferred_element_type=F32)
+    full, last = slice(0, 256), slice(256, 320)
+    gb[...] = jnp.dot(lb[...].astype(BF16), e2_ref[0:128, :], preferred_element_type=F32)
+    ga[full, :] = jnp.dot(la[full, :].astype(BF16), e1_ref[...], preferred_element_type=F32)
+    yy[full, :] = jnp.dot(ly[full, :].astype(BF16), ey_ref[...], preferred_element_type=F32)
+    ga[last, 0:LANES] = jnp.dot(la[last, :].astype(BF16), e2_ref[128:256, :], preferred_element_type=F32)
+    yy[last, 0:LANES] = jnp.dot(ly[last, :].astype(BF16), ey_ref[:, 0:LANES], preferred_element_type=F32)
     for g in range(SLOT_GROUPS):
-        r1, r2, dy = ends[g]
+        lone = g == SLOT_GROUPS - 1
+        r2 = ends_ref[40 + 8 * g : 48 + 8 * g, :]
         for c in range(CHANS):
-            at_rows = [slice(8 * ((2 * g + c) * 4 + b), 8 * ((2 * g + c) * 4 + b) + 8) for b in range(4)]
+            at_rows = [slice(64 * g + 32 * c + 8 * b, 64 * g + 32 * c + 8 * b + 8) for b in range(4)]
             gbr, gbi, dbr, dbi = [gb[r, :] for r in at_rows]
-            both = slice(16 * (2 * g + c), 16 * (2 * g + c) + 16)
             s_re = s_im = None
-            for j in range(8):
+            for j in range(1 if lone else 8):
                 cols = slice(LANES * j, LANES * j + LANES)
                 ga_r, ga_i, da_r, da_i = [ga[r, cols] for r in at_rows]
                 y_r, y_i, t_r, t_i = [yy[r, cols] for r in at_rows]
@@ -267,7 +283,7 @@
                 for x, dest in ((f, xf), (d, xd)):
                     for k in range(PARTS):
                         part = x.astype(BF16)
-                        dest[k, both, cols] = part
+                        dest[part_rows(g, c, k), cols] = part
                         if k + 1 < PARTS:
                             x = x - part.astype(F32)
                 s_re = a_r if j == 0 else s_re + a_r
@@ -277,19 +293,22 @@
                 one = one + pltpu.roll(one, 32, axis=1)
                 dest = slice(LANES * (2 * p + c), LANES * (2 * p + c + 1))
                 ff[40 + 8 * g : 48 + 8 * g, dest] = jnp.where((r2 & 3) == quad, one, 0.0)
-    first = jnp.dot(xf[0], s1_ref[...], preferred_element_type=F32)
-    diag = jnp.dot(xd[0], sd_ref[...], preferred_element_type=F32)
-    for k in range(1, PARTS):
-        first = first + jnp.dot(xf[k], s1_ref[...], preferred_element_type=F32)
-        diag = diag + jnp.dot(xd[k], sd_ref[...], preferred_element_type=F32)
+    first = [sums(slice(0, 256), 1024, xf, s1_ref), sums(slice(256, 320), LANES, xf, s1_ref)]
+    diag = [sums(slice(0, 256), 1024, xd, sd_ref), sums(slice(256, 320), LANES, xd, sd_ref)]
     for g in range(SLOT_GROUPS):
-        r1, r2, dy = ends[g]
+        r1 = ends_ref[8 * g : 8 * g + 8, :]
+        dy = ends_ref[80 + 8 * g : 88 + 8 * g, :]
         for c in range(CHANS):
             for p in range(2):
-                rows = slice(16 * (2 * g + c) + 8 * p, 16 * (2 * g + c) + 8 * p + 8)
+                at = 32 * (g % 4) + 16 * c + 8 * p
                 dest = slice(LANES * (2 * p + c), LANES * (2 * p + c + 1))
-                ff[8 * g : 8 * g + 8, dest] = jnp.where((r1 & 3) == quad, first[rows], 0.0)
-                gg[8 * g : 8 * g + 8, dest] = jnp.where((dy & 1) == half, diag[rows], 0.0)
+                f, d = first[g // 4][at : at + 8], diag[g // 4][at : at + 8]
+                if g == SLOT_GROUPS - 1:
+                    f = pltpu.roll(f, 0, axis=1, stride=4, stride_axis=0)
+                    for bit in (1, 2, 4):
+                        d = jnp.where((sub & bit) != 0, pltpu.roll(d, 64 - 4 * bit, axis=1), d)
+                ff[8 * g : 8 * g + 8, dest] = jnp.where((r1 & 3) == quad, f, 0.0)
+                gg[8 * g : 8 * g + 8, dest] = jnp.where((dy & 1) == half, d, 0.0)
     gsum = ysum = None
     for fx, gx in zip(split3(ff[...]), split3(gg[...])):
         fk = jnp.dot(hot_ref[0:16, 0:80], fx.astype(BF16), preferred_element_type=F32)
@@ -370,7 +389,7 @@
     after = lax.ppermute(gain_tan[:, 0:1], "tf", down)
     dish_table = dish_of.reshape(8, LANES)
     group_table = jnp.pad(group_of, (0, 16 * LANES - GROUPS)).reshape(16, LANES)
-    turned = jnp.pad(block_list.T, ((0, 0), (0, LANES - SLOTS)))
+    turned = jnp.pad(block_list.T, ((0, 0), (0, LANES - SLOTS)), mode="edge")
     tables = pl.pallas_call(
         prep_kernel,
         in_specs=vmem(5),
@@ -381,7 +400,7 @@
             pltpu.VMEM((8 * SLOT_GROUPS, 1024), F32),
             pltpu.VMEM((32, LANES), BF16),
             pltpu.VMEM((LANES, 1024), BF16),
-            pltpu.VMEM((LANES, LANES), BF16),
+            pltpu.VMEM((2 * LANES, LANES), BF16),
             pltpu.VMEM((2 * LANES, 1024), BF16),
             pltpu.VMEM((1024, LANES), BF16),
             pltpu.VMEM((1024, LANES), BF16),
@@ -403,8 +422,8 @@
             pltpu.VMEM((ROWS_ALL, 1024), F32),
             pltpu.VMEM((ROWS_ALL, LANES), F32),
             pltpu.VMEM((ROWS_ALL, 1024), F32),
-            pltpu.VMEM((PARTS, ROWS_ALL // 2, 1024), BF16),
-            pltpu.VMEM((PARTS, ROWS_ALL // 2, 1024), BF16),
+            pltpu.VMEM((PARTS * ROWS_ALL // 2, 1024), BF16),
+            pltpu.VMEM((PARTS * ROWS_ALL // 2, 1024), BF16),
             pltpu.VMEM((80, 4 * LANES), F32),
             pltpu.VMEM((40, 4 * LANES), F32),
             pltpu.VMEM((8, 4 * LANES), F32),

time: 50.3 us -> 50.1 us (level)
  other arithmetic: 0 us -> 0.64 us
    concatenate x0 -> x1, other arithmetic: none -> 0.64 us  [local(): turned = jnp.pad(block_list.T, ((0, 0), (0, LANES - SLOTS)), mode='edge')]
    pad x1 -> x0, local copies, waits for them, and re-layouts: 0.57 us -> none  [local(): turned = jnp.pad(block_list.T, ((0, 0), (0, LANES - SLOTS)))]
where the time goes in v5:
time: 50.1 us; the launch traced here: 49.8 us
  starting transfers between devices  29.4 us (59%)
  waiting for transfers between devices  9.99 us (20%)
  Pallas kernels  7.43 us (15%)
  local copies, waits for them, and re-layouts  1.58 us (3%)
  between operations  0.68 us (1%)
  other arithmetic  0.64 us (1%)
    all_to_all x2, starting transfers between devices, exchange(): return lax.all_to_all(x, 'bl', 0, 0, axis_index_groups=order, tiled=True)  23.2 us
    ppermute x1, waiting for transfers between devices, local(): after = lax.ppermute(gain_tan[:, 0:1], 'tf', down)  5.06 us
    all_to_all x2, waiting for transfers between devices, exchange(): return lax.all_to_all(x, 'bl', 0, 0, axis_index_groups=order, tiled=True)  4.92 us
    ppermute x1, starting transfers between devices, local(): before = lax.ppermute(gain_tan[:, 1:2], 'tf', up)  4.32 us
    pallas_call x1, Pallas kernels, local(): pl.pallas_call(main_kernel, in_specs=vmem(10), out_specs=vmem(1)[0], out_...  3.5 us
    ppermute x1, starting transfers between devices, local(): after = lax.ppermute(gain_tan[:, 0:1], 'tf', down)  1.92 us
    pallas_call x1, Pallas kernels, local(): pl.pallas_call(prep_kernel, in_specs=vmem(5), out_specs=vmem(9), out_shap...  1.75 us
    pallas_call x1, Pallas kernels, local(): pl.pallas_call(pack_kernel, in_specs=vmem(4), out_specs=vmem(1)[0], out_s...  1.45 us
  transfers between devices with their start and end apart: 4, of which 2 were waited for; matrix products, arithmetic and copies ran while one was open for 4% of the time, Pallas kernels for 4%

profile of v5, /device:TPU:25, one launch (start us, length us, event | category | flops | bytes accessed | tf_op | source)
XLA Modules:
  0.0 49.8 jit_solution(17369485898778203634)
XLA Ops:
  0.6 1.5 %pack.1 = f32[16,1,1536]{2,1,0:T(1,128)} custom-call(f32[2,2,64]{2,1,0:T(2,128)} %gain_ref.1, f32[2,2,64]{2,1,0:T(2,128)} %tan_ref.3, f32[2,2,124]{2,1,0:T(2,128)} %vis_ref.1, f32[2,2,124]{2,1,0:T(2,128)} %gtan_ref.1), custom_call_target="tpu_custom_call" | custom-call | tf_op jit(solution)/shard_map/pack/pallas_call | solution.py:377
  2.1 0.0 copy-start.2
  2.1 15.2 %all-to-all-start = ((f32[16,1,1536]{2,1,0:T(1,128)}), f32[16,1,1536]{2,1,0:T(1,128)S(1)}, u32[]{:S(2)}, u32[]{:S(2)}) async-start(f32[16,1,1536]{2,1,0:T(1,128)} %pack.1), calls=%async_computation | async-start | bytes 196608 | tf_op jit(solution)/shard_map/all_to_all | solution.py:372
  17.3 0.0 copy-done.2
  17.3 0.7 %copy.11.blocks_ref = s32[33,2]{1,0:T(8,128)} copy(s32[33,2]{0,1:T(2,128)S(1)} %copy-done.2) | data formatting | bytes 528 | tf_op args[6]
  18.0 0.0 copy-start.1
  18.0 0.2 slice_reduce_fusion
  18.2 0.1 reshape.17
  18.3 0.6 %pad_add_fusion.turned_ref = s32[2,128]{1,0:T(2,128)} fusion(s32[2,95]{1,0:T(2,128)S(1)} %reshape.17, s32[2,33]{1,0:T(2,128)S(1)} %bitcast.6), kind=kLoop, calls=%fused_computation.1 | loop fusion | flops 256 | bytes 2048 | tf_op jit(solution)/shard_map/jit(_pad)/concatenate | solution.py:392
  18.9 0.0 copy-done.1
  18.9 0.6 %pad_bitcast_fusion.group_ref = s32[16,128]{1,0:T(8,128)} fusion(s32[1984]{0:T(1024)S(1)} %copy-done.1), kind=kLoop, calls=%fused_computation | loop fusion | bytes 16128 | tf_op jit(solution)/shard_map/reshape | solution.py:391
  19.5 1.7 %prep.1 = (s32[96,128]{1,0:T(8,128)S(1)}, s32[120,128]{1,0:T(8,128)S(1)}, f32[40,1024]{1,0:T(8,128)S(1)}, bf16[32,128]{1,0:T(8,128)(2,1)S(1)}, bf16[128,1024]{1,...) custom-call(s32[8,128]{1,0:T(8,128)} %bitcast.4, ...), custom_call_target="tpu_custom_call" | custom-call | tf_op jit(solution)/shard_map/prep/pallas_call | solution.py:393
  21.3 4.9 %all-to-all-done.recv_ref = f32[16,1,1536]{2,1,0:T(1,128)S(1)} async-done(((f32[16,1,1536]{2,1,0:T(1,128)}), f32[16,1,1536]{2,1,0:T(1,128)S(1)}, u32[]{:S(2)}, u32[]{:S(2)}) %all-to-all-start) | async-done | bytes 98336 | tf_op jit(solution)/shard_map/all_to_all | solution.py:372
  26.2 3.5 %main.1 = f32[16,1,768]{2,1,0:T(1,128)} custom-call(f32[16,1,1536]{2,1,0:T(1,128)S(1)} %all-to-all-done.recv_ref, s32[96,128]{1,0:T(8,128)S(1)} %get-tuple-element.11.idx_ref, s32[120,128]{1,0:T(8,128)S(1)} %get-tuple-element.12.ends_ref, f32[40,1024]{1,0:T(8,128)S(1)} %get-tuple-element.13.wts_ref, bf16[32,128]{1,0:T(8,128)(2,1)S(1)} %get-tuple-element.14.hot_ref, ...), custom_call_target="tpu_custom_call" | custom-call | tf_op jit(solution)/shard_map/main/pallas_call | solution.py:410
  29.7 0.0 copy-start
  29.7 8.0 %all-to-all-start.1 = ((f32[16,1,768]{2,1,0:T(1,128)}), f32[16,1,768]{2,1,0:T(1,128)S(1)}, u32[]{:S(2)}, u32[]{:S(2)}) async-start(f32[16,1,768]{2,1,0:T(1,128)} %main.1), calls=%async_computation.1 | async-start | bytes 98304 | tf_op jit(solution)/shard_map/all_to_all | solution.py:372
  37.7 0.0 copy-done
  37.7 4.3 %collective-permute-start = (f32[2,1,64]{2,1,0:T(1,128)S(1)}, f32[2,1,64]{2,1,0:T(1,128)S(1)}, u32[]{:S(2)}, u32[]{:S(2)}) collective-permute-start(f32[2,1,64]{2,1,0:T(1,128)S(1)} %get-tuple-element.21), channel_id=1, source_target_pairs={{0,16},{16,32},{32,48},{48,64},{64,80},{80,96},{96,112},{112,128},... | collective-permute-start | bytes 1544 | tf_op jit(solution)/shard_map/ppermute | solution.py:388
  42.0 1.9 %collective-permute-start.1 = (f32[2,1,64]{2,1,0:T(1,128)S(1)}, f32[2,1,64]{2,1,0:T(1,128)S(1)}, u32[]{:S(2)}, u32[]{:S(2)}) collective-permute-start(f32[2,1,64]{2,1,0:T(1,128)S(1)} %get-tuple-element.20), channel_id=1, source_target_pairs={{16,0},{32,16},{48,32},{64,48},{80,64},{96,80},{112,96},{128,112},... | collective-permute-start | bytes 1544 | tf_op jit(solution)/shard_map/ppermute | solution.py:389
  44.0 0.0 collective-permute-done.before_ref
  44.0 5.1 %collective-permute-done.1.after_ref = f32[2,1,64]{2,1,0:T(1,128)S(1)} collective-permute-done((f32[2,1,64]{2,1,0:T(1,128)S(1)}, f32[2,1,64]{2,1,0:T(1,128)S(1)}, u32[]{:S(2)}, u32[]{:S(2)}) %collective-permute-start.1) | collective-permute-done | bytes 544 | tf_op jit(solution)/shard_map/ppermute | solution.py:389
  49.0 0.0 all-to-all-done.1.recv_ref
  49.0 0.7 %finish.1 = (f32[2,2,64]{2,1,0:T(2,128)}, f32[2,2,124]{2,1,0:T(2,128)}) custom-call(f32[16,1,768]{2,1,0:T(1,128)S(1)} %all-to-all-done.1.recv_ref, f32[2,2,64]{2,1,0:T(2,128)S(1)} %copy-done, f32[2,1,64]{2,1,0:T(1,128)S(1)} %collective-permute-done.before_ref, f32[2,1,64]{2,1,0:T(1,128)S(1)} %collective-permute-done.1.after_ref), custom_call_target="tpu_custom_call" | custom-call | tf_op jit(solution)/shard_map/finish/pallas_call | solution.py:435
  (1 shorter events, 0.0 us)
Async XLA Ops:
  2.1 15.2 %copy-start.2 = (s32[33,2]{0,1:T(2,128)S(1)}, s32[33,2]{0,1:T(2,128)}, u32[]{:S(2)}) copy-start(s32[33,2]{0,1:T(2,128)} %param.14) | copy-start | bytes 796
  2.1 24.1 %all-to-all-start = ((f32[16,1,1536]{2,1,0:T(1,128)}), f32[16,1,1536]{2,1,0:T(1,128)S(1)}, u32[]{:S(2)}, u32[]{:S(2)}) async-start(f32[16,1,1536]{2,1,0:T(1,128)} %pack.1), calls=%async_computation | async-start | bytes 196608 | tf_op jit(solution)/shard_map/all_to_all | solution.py:372
  18.0 0.9 %copy-start.1 = (s32[1984]{0:T(1024)S(1)}, s32[1984]{0:T(1024)}, u32[]{:S(2)}) copy-start(s32[1984]{0:T(1024)} %param.13) | copy-start | bytes 23812
  29.7 8.0 %copy-start = (f32[2,2,64]{2,1,0:T(2,128)S(1)}, f32[2,2,64]{2,1,0:T(2,128)}, u32[]{:S(2)}) copy-start(f32[2,2,64]{2,1,0:T(2,128)} %tan_ref.3) | copy-start | bytes 3076
  29.7 19.3 %all-to-all-start.1 = ((f32[16,1,768]{2,1,0:T(1,128)}), f32[16,1,768]{2,1,0:T(1,128)S(1)}, u32[]{:S(2)}, u32[]{:S(2)}) async-start(f32[16,1,768]{2,1,0:T(1,128)} %main.1), calls=%async_computation.1 | async-start | bytes 98304 | tf_op jit(solution)/shard_map/all_to_all | solution.py:372
  37.7 6.3 %collective-permute-start = (f32[2,1,64]{2,1,0:T(1,128)S(1)}, f32[2,1,64]{2,1,0:T(1,128)S(1)}, u32[]{:S(2)}, u32[]{:S(2)}) collective-permute-start(f32[2,1,64]{2,1,0:T(1,128)S(1)} %get-tuple-element.21), channel_id=1, source_target_pairs={{0,16},{16,32},{32,48},{48,64},{64,80},{80,96},{96,112},{112,128},... | collective-permute-start | bytes 1544 | tf_op jit(solution)/shard_map/ppermute | solution.py:388
  42.0 7.0 %collective-permute-start.1 = (f32[2,1,64]{2,1,0:T(1,128)S(1)}, f32[2,1,64]{2,1,0:T(1,128)S(1)}, u32[]{:S(2)}, u32[]{:S(2)}) collective-permute-start(f32[2,1,64]{2,1,0:T(1,128)S(1)} %get-tuple-element.20), channel_id=1, source_target_pairs={{16,0},{32,16},{48,32},{64,48},{80,64},{96,80},{112,96},{128,112},... | collective-permute-start | bytes 1544 | tf_op jit(solution)/shard_map/ppermute | solution.py:389

commit v6 on v5

--- a/solution.py
+++ b/solution.py
@@ -84,7 +84,7 @@
 
 def prep_kernel(
     dish_ref, group_ref, blocks_ref, turned_ref, weights_ref,
-    idx_ref, ends_ref, wts_ref, hot_ref, e1_ref, e2_ref, ey_ref, s1_ref, sd_ref,
+    idx_ref, ends_ref, wts_ref, hot_ref, e1_ref, e2_ref, ey_ref, s1_ref, sd_ref, pick_ref,
 ):
     lane = iota((8, LANES), 1)
     sub = iota((8, LANES), 0)
@@ -105,6 +105,11 @@
         zg = div124(found)
         idx_ref[8 * half : 8 * half + 8, :] = jnp.where(ok, place(zg), -1)
         idx_ref[16 + 8 * half : 24 + 8 * half, :] = found - 124 * zg
+    for r in range(16):
+        take = spread(idx_ref[16 + r : 17 + r, :], LANES) == iota((LANES, LANES), 0)
+        take = jnp.where(take, 1.0, 0.0).astype(BF16)
+        for part in range(2):
+            pick_ref[LANES * part : LANES * part + LANES, LANES * r : LANES * r + LANES] = take
     peer = iota((PEERS, LANES), 0)
     low = iota((LANES, LANES), 0)
     nt = (((1,), (1,)), ((), ()))
@@ -185,9 +190,9 @@
 
 
 def main_kernel(
-    recv_ref, idx_ref, ends_ref, wts_ref, hot_ref, e1_ref, e2_ref, ey_ref, s1_ref, sd_ref,
+    recv_ref, idx_ref, ends_ref, wts_ref, hot_ref, e1_ref, e2_ref, ey_ref, s1_ref, sd_ref, pick_ref,
     out_ref,
-    gsrc, gtab, ytab, la, lb, ly, ga, gb, yy, xf, xd, ff, gg, gout, yout,
+    lx, taken, gsrc, gtab, ytab, la, lb, ly, ga, gb, yy, xf, xd, ff, gg, gout, yout,
 ):
     lane = iota((8, LANES), 1)
     quad = lane >> 5
@@ -205,15 +210,18 @@
         for k in range(1, 8):
             res = jnp.where(at_row == k, by_lane(spread(gsrc[q, k : k + 1, :]), at_lane), res)
         gtab[q] = res
-    for b in range(8):
-        res = [jnp.zeros((8, LANES), F32), jnp.zeros((8, LANES), F32)]
-        for z in range(PEERS):
-            row = spread(recv_ref[z, :, 512 + LANES * b : 512 + LANES * b + LANES])
-            for h in range(2):
-                hit = idx_ref[8 * h : 8 * h + 8, :] == z
-                res[h] = jnp.where(hit, by_lane(row, idx_ref[16 + 8 * h : 24 + 8 * h, :]), res[h])
-        ytab[b, 0:8, :] = res[0]
-        ytab[b, 8:16, :] = res[1]
+    for q in range(8):
+        x = recv_ref[:, 0, 512 + LANES * q : 512 + LANES * q + LANES]
+        part = x.astype(BF16)
+        lx[16 * q : 16 * q + 16, 0:128] = part
+        lx[16 * q : 16 * q + 16, 128:256] = (x - part.astype(F32)).astype(BF16)
+    taken[...] = jnp.dot(lx[...], pick_ref[...], preferred_element_type=F32)
+    peer = iota((PEERS, LANES), 0)
+    for r in range(16):
+        hit = spread(idx_ref[r : r + 1, :], PEERS) == peer
+        for q in range(8):
+            x = jnp.where(hit, taken[16 * q : 16 * q + 16, LANES * r : LANES * r + LANES], 0.0)
+            ytab[q, r : r + 1, :] = jnp.sum(x, axis=0, keepdims=True)
     def part_rows(g, c, k):
         at = 128 * k + 32 * g + 16 * c if g < 4 else 256 + 32 * k + 16 * c
         return slice(at, at + 16)
@@ -393,7 +401,7 @@
     tables = pl.pallas_call(
         prep_kernel,
         in_specs=vmem(5),
-        out_specs=vmem(9),
+        out_specs=vmem(10),
         out_shape=(
             pltpu.VMEM((96, LANES), I32),
             pltpu.VMEM((120, LANES), I32),
@@ -404,15 +412,18 @@
             pltpu.VMEM((2 * LANES, 1024), BF16),
             pltpu.VMEM((1024, LANES), BF16),
             pltpu.VMEM((1024, LANES), BF16),
+            pltpu.VMEM((2 * LANES, 16 * LANES), BF16),
         ),
         name="prep",
     )(dish_table, group_table, block_list, turned, weights)
     partial = pl.pallas_call(
         main_kernel,
-        in_specs=vmem(10),
+        in_specs=vmem(11),
         out_specs=vmem(1)[0],
         out_shape=pltpu.VMEM((PEERS, 1, SCATTER_WIDTH), F32),
         scratch_shapes=[
+            pltpu.VMEM((LANES, 2 * LANES), BF16),
+            pltpu.VMEM((LANES, 16 * LANES), F32),
             pltpu.VMEM((8, 8, LANES), F32),
             pltpu.VMEM((8, 8, LANES), F32),
             pltpu.VMEM((8, 16, LANES), F32),

time: 50.1 us -> 49.8 us (level)
  no operation moved by 1% of the time
where the time goes in v6:
time: 49.8 us; the launch traced here: 49.5 us
  starting transfers between devices  29.5 us (59%)
  waiting for transfers between devices  9.69 us (19%)
  Pallas kernels  7.43 us (15%)
  local copies, waits for them, and re-layouts  1.58 us (3%)
  between operations  0.68 us (1%)
  other arithmetic  0.64 us (1%)
    all_to_all x2, starting transfers between devices, exchange(): return lax.all_to_all(x, 'bl', 0, 0, axis_index_groups=order, tiled=True)  23.2 us
    ppermute x1, waiting for transfers between devices, local(): after = lax.ppermute(gain_tan[:, 0:1], 'tf', down)  5.06 us
    all_to_all x2, waiting for transfers between devices, exchange(): return lax.all_to_all(x, 'bl', 0, 0, axis_index_groups=order, tiled=True)  4.62 us
    ppermute x1, starting transfers between devices, local(): before = lax.ppermute(gain_tan[:, 1:2], 'tf', up)  4.33 us
    pallas_call x1, Pallas kernels, local(): pl.pallas_call(main_kernel, in_specs=vmem(11), out_specs=vmem(1)[0], out_...  3.21 us
    pallas_call x1, Pallas kernels, local(): pl.pallas_call(prep_kernel, in_specs=vmem(5), out_specs=vmem(10), out_sha...  2.05 us
    ppermute x1, starting transfers between devices, local(): after = lax.ppermute(gain_tan[:, 0:1], 'tf', down)  1.92 us
    pallas_call x1, Pallas kernels, local(): pl.pallas_call(pack_kernel, in_specs=vmem(4), out_specs=vmem(1)[0], out_s...  1.45 us
  transfers between devices with their start and end apart: 4, of which 2 were waited for; matrix products, arithmetic and copies ran while one was open for 4% of the time, Pallas kernels for 4%

profile of v6, /device:TPU:25, one launch (start us, length us, event | category | flops | bytes accessed | tf_op | source)
XLA Modules:
  0.0 49.5 jit_solution(6498793408992579594)
XLA Ops:
  0.6 1.5 %pack.1 = f32[16,1,1536]{2,1,0:T(1,128)} custom-call(f32[2,2,64]{2,1,0:T(2,128)} %gain_ref.1, f32[2,2,64]{2,1,0:T(2,128)} %tan_ref.3, f32[2,2,124]{2,1,0:T(2,128)} %vis_ref.1, f32[2,2,124]{2,1,0:T(2,128)} %gtan_ref.1), custom_call_target="tpu_custom_call" | custom-call | tf_op jit(solution)/shard_map/pack/pallas_call | solution.py:385
  2.1 0.0 copy-start.2
  2.1 15.2 %all-to-all-start = ((f32[16,1,1536]{2,1,0:T(1,128)}), f32[16,1,1536]{2,1,0:T(1,128)S(1)}, u32[]{:S(2)}, u32[]{:S(2)}) async-start(f32[16,1,1536]{2,1,0:T(1,128)} %pack.1), calls=%async_computation | async-start | bytes 196608 | tf_op jit(solution)/shard_map/all_to_all | solution.py:380
  17.3 0.0 copy-done.2
  17.3 0.7 %copy.11.blocks_ref = s32[33,2]{1,0:T(8,128)} copy(s32[33,2]{0,1:T(2,128)S(1)} %copy-done.2) | data formatting | bytes 528 | tf_op args[6]
  18.0 0.0 copy-start.1
  18.0 0.2 slice_reduce_fusion
  18.2 0.1 reshape.17
  18.3 0.6 %pad_add_fusion.turned_ref = s32[2,128]{1,0:T(2,128)} fusion(s32[2,95]{1,0:T(2,128)S(1)} %reshape.17, s32[2,33]{1,0:T(2,128)S(1)} %bitcast.6), kind=kLoop, calls=%fused_computation.1 | loop fusion | flops 256 | bytes 2048 | tf_op jit(solution)/shard_map/jit(_pad)/concatenate | solution.py:400
  18.9 0.0 copy-done.1
  18.9 0.6 %pad_bitcast_fusion.group_ref = s32[16,128]{1,0:T(8,128)} fusion(s32[1984]{0:T(1024)S(1)} %copy-done.1), kind=kLoop, calls=%fused_computation | loop fusion | bytes 16128 | tf_op jit(solution)/shard_map/reshape | solution.py:399
  19.5 2.0 %prep.1 = (s32[96,128]{1,0:T(8,128)S(1)}, s32[120,128]{1,0:T(8,128)S(1)}, f32[40,1024]{1,0:T(8,128)S(1)}, bf16[32,128]{1,0:T(8,128)(2,1)S(1)}, bf16[128,1024]{1,...) custom-call(s32[8,128]{1,0:T(8,128)} %bitcast.4, ...), custom_call_target="tpu_custom_call" | custom-call | tf_op jit(solution)/shard_map/prep/pallas_call | solution.py:401
  21.6 4.6 %all-to-all-done.recv_ref = f32[16,1,1536]{2,1,0:T(1,128)S(1)} async-done(((f32[16,1,1536]{2,1,0:T(1,128)}), f32[16,1,1536]{2,1,0:T(1,128)S(1)}, u32[]{:S(2)}, u32[]{:S(2)}) %all-to-all-start) | async-done | bytes 98336 | tf_op jit(solution)/shard_map/all_to_all | solution.py:380
  26.2 3.2 %main.1 = f32[16,1,768]{2,1,0:T(1,128)} custom-call(f32[16,1,1536]{2,1,0:T(1,128)S(1)} %all-to-all-done.recv_ref, s32[96,128]{1,0:T(8,128)S(1)} %get-tuple-element.12.idx_ref, s32[120,128]{1,0:T(8,128)S(1)} %get-tuple-element.13.ends_ref, f32[40,1024]{1,0:T(8,128)S(1)} %get-tuple-element.14.wts_ref, bf16[32,128]{1,0:T(8,128)(2,1)S(1)} %get-tuple-element.15.hot_ref, ...), custom_call_target="tpu_custom_call" | custom-call | tf_op jit(solution)/shard_map/main/pallas_call | solution.py:419
  29.4 0.0 copy-start
  29.4 8.0 %all-to-all-start.1 = ((f32[16,1,768]{2,1,0:T(1,128)}), f32[16,1,768]{2,1,0:T(1,128)S(1)}, u32[]{:S(2)}, u32[]{:S(2)}) async-start(f32[16,1,768]{2,1,0:T(1,128)} %main.1), calls=%async_computation.1 | async-start | bytes 98304 | tf_op jit(solution)/shard_map/all_to_all | solution.py:380
  37.4 0.0 copy-done
  37.4 4.3 %collective-permute-start = (f32[2,1,64]{2,1,0:T(1,128)S(1)}, f32[2,1,64]{2,1,0:T(1,128)S(1)}, u32[]{:S(2)}, u32[]{:S(2)}) collective-permute-start(f32[2,1,64]{2,1,0:T(1,128)S(1)} %get-tuple-element.23), channel_id=1, source_target_pairs={{0,16},{16,32},{32,48},{48,64},{64,80},{80,96},{96,112},{112,128},... | collective-permute-start | bytes 1544 | tf_op jit(solution)/shard_map/ppermute | solution.py:396
  41.7 1.9 %collective-permute-start.1 = (f32[2,1,64]{2,1,0:T(1,128)S(1)}, f32[2,1,64]{2,1,0:T(1,128)S(1)}, u32[]{:S(2)}, u32[]{:S(2)}) collective-permute-start(f32[2,1,64]{2,1,0:T(1,128)S(1)} %get-tuple-element.22), channel_id=1, source_target_pairs={{16,0},{32,16},{48,32},{64,48},{80,64},{96,80},{112,96},{128,112},... | collective-permute-start | bytes 1544 | tf_op jit(solution)/shard_map/ppermute | solution.py:397
  43.7 0.0 collective-permute-done.before_ref
  43.7 5.1 %collective-permute-done.1.after_ref = f32[2,1,64]{2,1,0:T(1,128)S(1)} collective-permute-done((f32[2,1,64]{2,1,0:T(1,128)S(1)}, f32[2,1,64]{2,1,0:T(1,128)S(1)}, u32[]{:S(2)}, u32[]{:S(2)}) %collective-permute-start.1) | collective-permute-done | bytes 544 | tf_op jit(solution)/shard_map/ppermute | solution.py:397
  48.7 0.0 all-to-all-done.1.recv_ref
  48.7 0.7 %finish.1 = (f32[2,2,64]{2,1,0:T(2,128)}, f32[2,2,124]{2,1,0:T(2,128)}) custom-call(f32[16,1,768]{2,1,0:T(1,128)S(1)} %all-to-all-done.1.recv_ref, f32[2,2,64]{2,1,0:T(2,128)S(1)} %copy-done, f32[2,1,64]{2,1,0:T(1,128)S(1)} %collective-permute-done.before_ref, f32[2,1,64]{2,1,0:T(1,128)S(1)} %collective-permute-done.1.after_ref), custom_call_target="tpu_custom_call" | custom-call | tf_op jit(solution)/shard_map/finish/pallas_call | solution.py:446
  (1 shorter events, 0.0 us)
Async XLA Ops:
  2.1 15.2 %copy-start.2 = (s32[33,2]{0,1:T(2,128)S(1)}, s32[33,2]{0,1:T(2,128)}, u32[]{:S(2)}) copy-start(s32[33,2]{0,1:T(2,128)} %param.14) | copy-start | bytes 796
  2.1 24.1 %all-to-all-start = ((f32[16,1,1536]{2,1,0:T(1,128)}), f32[16,1,1536]{2,1,0:T(1,128)S(1)}, u32[]{:S(2)}, u32[]{:S(2)}) async-start(f32[16,1,1536]{2,1,0:T(1,128)} %pack.1), calls=%async_computation | async-start | bytes 196608 | tf_op jit(solution)/shard_map/all_to_all | solution.py:380
  18.0 0.9 %copy-start.1 = (s32[1984]{0:T(1024)S(1)}, s32[1984]{0:T(1024)}, u32[]{:S(2)}) copy-start(s32[1984]{0:T(1024)} %param.13) | copy-start | bytes 23812
  29.4 8.0 %copy-start = (f32[2,2,64]{2,1,0:T(2,128)S(1)}, f32[2,2,64]{2,1,0:T(2,128)}, u32[]{:S(2)}) copy-start(f32[2,2,64]{2,1,0:T(2,128)} %tan_ref.3) | copy-start | bytes 3076
  29.4 19.3 %all-to-all-start.1 = ((f32[16,1,768]{2,1,0:T(1,128)}), f32[16,1,768]{2,1,0:T(1,128)S(1)}, u32[]{:S(2)}, u32[]{:S(2)}) async-start(f32[16,1,768]{2,1,0:T(1,128)} %main.1), calls=%async_computation.1 | async-start | bytes 98304 | tf_op jit(solution)/shard_map/all_to_all | solution.py:380
  37.4 6.3 %collective-permute-start = (f32[2,1,64]{2,1,0:T(1,128)S(1)}, f32[2,1,64]{2,1,0:T(1,128)S(1)}, u32[]{:S(2)}, u32[]{:S(2)}) collective-permute-start(f32[2,1,64]{2,1,0:T(1,128)S(1)} %get-tuple-element.23), channel_id=1, source_target_pairs={{0,16},{16,32},{32,48},{48,64},{64,80},{80,96},{96,112},{112,128},... | collective-permute-start | bytes 1544 | tf_op jit(solution)/shard_map/ppermute | solution.py:396
  41.7 7.0 %collective-permute-start.1 = (f32[2,1,64]{2,1,0:T(1,128)S(1)}, f32[2,1,64]{2,1,0:T(1,128)S(1)}, u32[]{:S(2)}, u32[]{:S(2)}) collective-permute-start(f32[2,1,64]{2,1,0:T(1,128)S(1)} %get-tuple-element.22), channel_id=1, source_target_pairs={{16,0},{32,16},{48,32},{64,48},{80,64},{96,80},{112,96},{128,112},... | collective-permute-start | bytes 1544 | tf_op jit(solution)/shard_map/ppermute | solution.py:397

commit v7 on v6

--- a/solution.py
+++ b/solution.py
@@ -21,7 +21,7 @@
 GATHER_WIDTH = 1536
 SCATTER_WIDTH = 768
 PARTS = 2
-LEAD = 12
+LEAD = 13
 STEP = 1
 UNSTEP = 1
 

time: 49.8 us -> 49.8 us (level)
  starting transfers between devices: 29.5 us -> 28.9 us
  waiting for transfers between devices: 9.69 us -> 10.2 us
    all_to_all x2, starting transfers between devices: 23.2 us -> 22.4 us  [exchange(): return lax.all_to_all(x, 'bl', 0, 0, axis_index_groups=order, tiled=True)]
    all_to_all x2, waiting for transfers between devices: 4.62 us -> 5.13 us  [exchange(): return lax.all_to_all(x, 'bl', 0, 0, axis_index_groups=order, tiled=True)]
where the time goes in v7:
time: 49.8 us; the launch traced here: 49.5 us
  starting transfers between devices  28.9 us (58%)
  waiting for transfers between devices  10.2 us (20%)
  Pallas kernels  7.44 us (15%)
  local copies, waits for them, and re-layouts  1.58 us (3%)
  between operations  0.68 us (1%)
  other arithmetic  0.64 us (1%)
    all_to_all x2, starting transfers between devices, exchange(): return lax.all_to_all(x, 'bl', 0, 0, axis_index_groups=order, tiled=True)  22.4 us
    all_to_all x2, waiting for transfers between devices, exchange(): return lax.all_to_all(x, 'bl', 0, 0, axis_index_groups=order, tiled=True)  5.13 us
    ppermute x1, waiting for transfers between devices, local(): after = lax.ppermute(gain_tan[:, 0:1], 'tf', down)  5.06 us
    ppermute x1, starting transfers between devices, local(): before = lax.ppermute(gain_tan[:, 1:2], 'tf', up)  4.57 us
    pallas_call x1, Pallas kernels, local(): pl.pallas_call(main_kernel, in_specs=vmem(11), out_specs=vmem(1)[0], out_...  3.22 us
    pallas_call x1, Pallas kernels, local(): pl.pallas_call(prep_kernel, in_specs=vmem(5), out_specs=vmem(10), out_sha...  2.05 us
    ppermute x1, starting transfers between devices, local(): after = lax.ppermute(gain_tan[:, 0:1], 'tf', down)  1.92 us
    pallas_call x1, Pallas kernels, local(): pl.pallas_call(pack_kernel, in_specs=vmem(4), out_specs=vmem(1)[0], out_s...  1.45 us
  transfers between devices with their start and end apart: 4, of which 2 were waited for; matrix products, arithmetic and copies ran while one was open for 4% of the time, Pallas kernels for 4%

profile of v7, /device:TPU:25, one launch (start us, length us, event | category | flops | bytes accessed | tf_op | source)
XLA Modules:
  0.0 49.5 jit_solution(9811063901905598694)
XLA Ops:
  0.6 1.5 %pack.1 = f32[16,1,1536]{2,1,0:T(1,128)} custom-call(f32[2,2,64]{2,1,0:T(2,128)} %gain_ref.1, f32[2,2,64]{2,1,0:T(2,128)} %tan_ref.3, f32[2,2,124]{2,1,0:T(2,128)} %vis_ref.1, f32[2,2,124]{2,1,0:T(2,128)} %gtan_ref.1), custom_call_target="tpu_custom_call" | custom-call | tf_op jit(solution)/shard_map/pack/pallas_call | solution.py:385
  2.1 0.0 copy-start.2
  2.1 15.2 %all-to-all-start = ((f32[16,1,1536]{2,1,0:T(1,128)}), f32[16,1,1536]{2,1,0:T(1,128)S(1)}, u32[]{:S(2)}, u32[]{:S(2)}) async-start(f32[16,1,1536]{2,1,0:T(1,128)} %pack.1), calls=%async_computation | async-start | bytes 196608 | tf_op jit(solution)/shard_map/all_to_all | solution.py:380
  17.3 0.0 copy-done.2
  17.3 0.7 %copy.11.blocks_ref = s32[33,2]{1,0:T(8,128)} copy(s32[33,2]{0,1:T(2,128)S(1)} %copy-done.2) | data formatting | bytes 528 | tf_op args[6]
  18.0 0.0 copy-start.1
  18.0 0.2 slice_reduce_fusion
  18.2 0.1 reshape.17
  18.3 0.6 %pad_add_fusion.turned_ref = s32[2,128]{1,0:T(2,128)} fusion(s32[2,95]{1,0:T(2,128)S(1)} %reshape.17, s32[2,33]{1,0:T(2,128)S(1)} %bitcast.6), kind=kLoop, calls=%fused_computation.1 | loop fusion | flops 256 | bytes 2048 | tf_op jit(solution)/shard_map/jit(_pad)/concatenate | solution.py:400
  18.9 0.0 copy-done.1
  18.9 0.6 %pad_bitcast_fusion.group_ref = s32[16,128]{1,0:T(8,128)} fusion(s32[1984]{0:T(1024)S(1)} %copy-done.1), kind=kLoop, calls=%fused_computation | loop fusion | bytes 16128 | tf_op jit(solution)/shard_map/reshape | solution.py:399
  19.5 2.0 %prep.1 = (s32[96,128]{1,0:T(8,128)S(1)}, s32[120,128]{1,0:T(8,128)S(1)}, f32[40,1024]{1,0:T(8,128)S(1)}, bf16[32,128]{1,0:T(8,128)(2,1)S(1)}, bf16[128,1024]{1,...) custom-call(s32[8,128]{1,0:T(8,128)} %bitcast.4, ...), custom_call_target="tpu_custom_call" | custom-call | tf_op jit(solution)/shard_map/prep/pallas_call | solution.py:401
  21.6 5.1 %all-to-all-done.recv_ref = f32[16,1,1536]{2,1,0:T(1,128)S(1)} async-done(((f32[16,1,1536]{2,1,0:T(1,128)}), f32[16,1,1536]{2,1,0:T(1,128)S(1)}, u32[]{:S(2)}, u32[]{:S(2)}) %all-to-all-start) | async-done | bytes 98336 | tf_op jit(solution)/shard_map/all_to_all | solution.py:380
  26.7 3.2 %main.1 = f32[16,1,768]{2,1,0:T(1,128)} custom-call(f32[16,1,1536]{2,1,0:T(1,128)S(1)} %all-to-all-done.recv_ref, s32[96,128]{1,0:T(8,128)S(1)} %get-tuple-element.12.idx_ref, s32[120,128]{1,0:T(8,128)S(1)} %get-tuple-element.13.ends_ref, f32[40,1024]{1,0:T(8,128)S(1)} %get-tuple-element.14.wts_ref, bf16[32,128]{1,0:T(8,128)(2,1)S(1)} %get-tuple-element.15.hot_ref, ...), custom_call_target="tpu_custom_call" | custom-call | tf_op jit(solution)/shard_map/main/pallas_call | solution.py:419
  29.9 0.0 copy-start
  29.9 7.2 %all-to-all-start.1 = ((f32[16,1,768]{2,1,0:T(1,128)}), f32[16,1,768]{2,1,0:T(1,128)S(1)}, u32[]{:S(2)}, u32[]{:S(2)}) async-start(f32[16,1,768]{2,1,0:T(1,128)} %main.1), calls=%async_computation.1 | async-start | bytes 98304 | tf_op jit(solution)/shard_map/all_to_all | solution.py:380
  37.1 0.0 copy-done
  37.2 4.6 %collective-permute-start = (f32[2,1,64]{2,1,0:T(1,128)S(1)}, f32[2,1,64]{2,1,0:T(1,128)S(1)}, u32[]{:S(2)}, u32[]{:S(2)}) collective-permute-start(f32[2,1,64]{2,1,0:T(1,128)S(1)} %get-tuple-element.23), channel_id=1, source_target_pairs={{0,16},{16,32},{32,48},{48,64},{64,80},{80,96},{96,112},{112,128},... | collective-permute-start | bytes 1544 | tf_op jit(solution)/shard_map/ppermute | solution.py:396
  41.7 1.9 %collective-permute-start.1 = (f32[2,1,64]{2,1,0:T(1,128)S(1)}, f32[2,1,64]{2,1,0:T(1,128)S(1)}, u32[]{:S(2)}, u32[]{:S(2)}) collective-permute-start(f32[2,1,64]{2,1,0:T(1,128)S(1)} %get-tuple-element.22), channel_id=1, source_target_pairs={{16,0},{32,16},{48,32},{64,48},{80,64},{96,80},{112,96},{128,112},... | collective-permute-start | bytes 1544 | tf_op jit(solution)/shard_map/ppermute | solution.py:397
  43.7 0.0 collective-permute-done.before_ref
  43.7 5.1 %collective-permute-done.1.after_ref = f32[2,1,64]{2,1,0:T(1,128)S(1)} collective-permute-done((f32[2,1,64]{2,1,0:T(1,128)S(1)}, f32[2,1,64]{2,1,0:T(1,128)S(1)}, u32[]{:S(2)}, u32[]{:S(2)}) %collective-permute-start.1) | collective-permute-done | bytes 544 | tf_op jit(solution)/shard_map/ppermute | solution.py:397
  48.7 0.0 all-to-all-done.1.recv_ref
  48.7 0.7 %finish.1 = (f32[2,2,64]{2,1,0:T(2,128)}, f32[2,2,124]{2,1,0:T(2,128)}) custom-call(f32[16,1,768]{2,1,0:T(1,128)S(1)} %all-to-all-done.1.recv_ref, f32[2,2,64]{2,1,0:T(2,128)S(1)} %copy-done, f32[2,1,64]{2,1,0:T(1,128)S(1)} %collective-permute-done.before_ref, f32[2,1,64]{2,1,0:T(1,128)S(1)} %collective-permute-done.1.after_ref), custom_call_target="tpu_custom_call" | custom-call | tf_op jit(solution)/shard_map/finish/pallas_call | solution.py:446
  (1 shorter events, 0.0 us)
Async XLA Ops:
  2.1 15.2 %copy-start.2 = (s32[33,2]{0,1:T(2,128)S(1)}, s32[33,2]{0,1:T(2,128)}, u32[]{:S(2)}) copy-start(s32[33,2]{0,1:T(2,128)} %param.14) | copy-start | bytes 796
  2.1 24.6 %all-to-all-start = ((f32[16,1,1536]{2,1,0:T(1,128)}), f32[16,1,1536]{2,1,0:T(1,128)S(1)}, u32[]{:S(2)}, u32[]{:S(2)}) async-start(f32[16,1,1536]{2,1,0:T(1,128)} %pack.1), calls=%async_computation | async-start | bytes 196608 | tf_op jit(solution)/shard_map/all_to_all | solution.py:380
  18.0 0.9 %copy-start.1 = (s32[1984]{0:T(1024)S(1)}, s32[1984]{0:T(1024)}, u32[]{:S(2)}) copy-start(s32[1984]{0:T(1024)} %param.13) | copy-start | bytes 23812
  29.9 7.2 %copy-start = (f32[2,2,64]{2,1,0:T(2,128)S(1)}, f32[2,2,64]{2,1,0:T(2,128)}, u32[]{:S(2)}) copy-start(f32[2,2,64]{2,1,0:T(2,128)} %tan_ref.3) | copy-start | bytes 3076
  29.9 18.8 %all-to-all-start.1 = ((f32[16,1,768]{2,1,0:T(1,128)}), f32[16,1,768]{2,1,0:T(1,128)S(1)}, u32[]{:S(2)}, u32[]{:S(2)}) async-start(f32[16,1,768]{2,1,0:T(1,128)} %main.1), calls=%async_computation.1 | async-start | bytes 98304 | tf_op jit(solution)/shard_map/all_to_all | solution.py:380
  37.2 6.5 %collective-permute-start = (f32[2,1,64]{2,1,0:T(1,128)S(1)}, f32[2,1,64]{2,1,0:T(1,128)S(1)}, u32[]{:S(2)}, u32[]{:S(2)}) collective-permute-start(f32[2,1,64]{2,1,0:T(1,128)S(1)} %get-tuple-element.23), channel_id=1, source_target_pairs={{0,16},{16,32},{32,48},{48,64},{64,80},{80,96},{96,112},{112,128},... | collective-permute-start | bytes 1544 | tf_op jit(solution)/shard_map/ppermute | solution.py:396
  41.7 7.0 %collective-permute-start.1 = (f32[2,1,64]{2,1,0:T(1,128)S(1)}, f32[2,1,64]{2,1,0:T(1,128)S(1)}, u32[]{:S(2)}, u32[]{:S(2)}) collective-permute-start(f32[2,1,64]{2,1,0:T(1,128)S(1)} %get-tuple-element.22), channel_id=1, source_target_pairs={{16,0},{32,16},{48,32},{64,48},{80,64},{96,80},{112,96},{128,112},... | collective-permute-start | bytes 1544 | tf_op jit(solution)/shard_map/ppermute | solution.py:397
